TPU v7x, 256 devices: a whole 4x4x8 slice. The times are simulated.
256 devices in a mesh: dp: 64 (over x, z, core), mp: 4 (over y).
Axes of the slice: x: 4, y: 4, z: 8, core: 2. Of those that a mesh axis runs over, the one named last changes fastest.
Arguments:
- query_rows: bfloat16 [16384, 2048], P('dp', 'mp'), may hold values from -6 to 6
- key_rows: bfloat16 [16384, 512], P('dp', 'mp'), may hold values from -6 to 6
- value_matrix: bfloat16 [16384, 512], P('dp', 'mp'), may hold values from -6 to 6
- out_weight: bfloat16 [2048, 5120], P('mp', 'dp'), may hold values from -0.125 to 0.125
- out_grad: bfloat16 [16384, 5120], P('dp', 'mp'), may hold values from -16 to 16
- doc_lengths: int32 [64, 8], P('dp'), may hold values from 1 to 249, as said below
Outputs:
- layer_out: bfloat16 [16384, 5120], P('dp', 'mp')
- query_grad: bfloat16 [16384, 2048], P('dp', 'mp')
- key_grad: bfloat16 [16384, 512], P('dp', 'mp')
- value_grad: bfloat16 [16384, 512], P('dp', 'mp')
- weight_grad: float32 [2048, 5120], P('mp', 'dp')
Inputs may be any that keep to these rules, and one draw needn't show every extreme that they name: `doc_lengths`: each row holds 8 lengths of 1 or more that sum to 256.
All inputs are finite; a program needn't handle non-finite values.
Results may differ from a plain program's by a relative error of at most 0.014.
Values may be sent and summed in bfloat16 or wider, within the bound.
No kernel may reach another device: no remote copies, remote signals or barrier semaphores. Data moves between devices by JAX's collectives and lax.ppermute only.
A program may use at most 64 MiB of HBM per device.

v0:
```python
import jax
import jax.numpy as jnp
from jax import lax
from jax.sharding import PartitionSpec as P

HEAD_WIDTH = 128
TILE = 128


def from_everyone(x, axis):
    size = lax.axis_size(axis)
    return lax.all_to_all(jnp.broadcast_to(x[None], (size, *x.shape)), axis, 0, 0, tiled=True)


def joined_along(pieces, dim):
    lengths = list(pieces.shape[1:])
    lengths[dim] *= pieces.shape[0]
    return jnp.moveaxis(pieces, 0, dim).reshape(lengths)


def collect(x, axis, dim):
    pieces = from_everyone(x, axis)
    return joined_along(pieces, dim)


def in_blocks(x, dim, size):
    lengths = x.shape
    pieces = x.reshape(*lengths[:dim], size, lengths[dim] // size, *lengths[dim + 1 :])
    return jnp.moveaxis(pieces, dim, 0)


def sum_at_owner(x, axis, dim):
    pieces = in_blocks(x, dim, lax.axis_size(axis))
    arrived = lax.all_to_all(pieces, axis, split_axis=0, concat_axis=0, tiled=True)
    return arrived.astype(jnp.float32).sum(axis=0)


def local_segments(lengths, row_count):
    segment_ends = jnp.cumsum(lengths)
    positions = jnp.arange(row_count, dtype=jnp.int32)
    return jnp.sum((positions[:, None] >= segment_ends[None, :]).astype(jnp.int32), axis=1)


def to_heads(matrix):
    return matrix.reshape(matrix.shape[0], matrix.shape[1] // HEAD_WIDTH, HEAD_WIDTH).transpose(
        1, 0, 2
    )


def from_heads(tensor):
    return tensor.transpose(1, 0, 2).reshape(tensor.shape[1], tensor.shape[0] * tensor.shape[2])


def attend(queries, key_rows, value_matrix, upstreams, segment):
    head_count, row_count, head_size = queries.shape
    tile_rows = min(TILE, row_count)
    block_count = row_count // tile_rows
    softmax_scale = HEAD_WIDTH ** (-0.5)
    offsets = jnp.arange(tile_rows, dtype=jnp.int32)
    empty_rows = jnp.zeros((tile_rows, head_size), jnp.float32)
    key_sums = [empty_rows] * block_count
    value_sums = [empty_rows] * block_count
    attended_blocks = []
    grad_blocks = []
    for block_index in range(block_count):
        row_start = block_index * tile_rows
        query_tile = queries[:, row_start : row_start + tile_rows]
        upstream_tile = upstreams[:, row_start : row_start + tile_rows]
        query_segment = segment[row_start : row_start + tile_rows]
        active = [
            segment[(column_index + 1) * tile_rows - 1] >= query_segment[0]
            for column_index in range(block_index + 1)
        ]
        score_tiles = []
        for column_index in range(block_index + 1):
            column_start = column_index * tile_rows
            key_tile = key_rows[column_start : column_start + tile_rows]
            key_segment = segment[column_start : column_start + tile_rows]
            allowed = (query_segment[:, None] == key_segment[None, :]) & (
                (row_start + offsets)[:, None] >= (column_start + offsets)[None, :]
            )

            def score_tile(query_tile=query_tile, key_tile=key_tile, allowed=allowed):
                logits = (
                    jnp.einsum(
                        "hid,jd->hij", query_tile, key_tile, preferred_element_type=jnp.float32
                    )
                    * softmax_scale
                )
                return jnp.where(allowed[None], logits, -jnp.inf)

            def masked_tile():
                return jnp.full((head_count, tile_rows, tile_rows), -jnp.inf, jnp.float32)

            score_tiles.append(lax.cond(active[column_index], score_tile, masked_tile))
        logits = jnp.concatenate(score_tiles, axis=-1)
        row_max = jnp.max(logits, axis=-1, keepdims=True)
        exp_terms = jnp.exp(logits - row_max)
        probability = exp_terms / jnp.sum(exp_terms, axis=-1, keepdims=True)
        weights = probability.astype(jnp.bfloat16)
        attended = jnp.zeros((head_count, tile_rows, head_size), jnp.float32)
        grad_tiles = []
        for column_index in range(block_index + 1):
            column_start = column_index * tile_rows
            value_tile = value_matrix[column_start : column_start + tile_rows]
            weight_tile = weights[:, :, column_start : column_start + tile_rows]

            def forward_tile(
                weight_tile=weight_tile, value_tile=value_tile, upstream_tile=upstream_tile
            ):
                return (
                    jnp.einsum(
                        "hij,jd->hid", weight_tile, value_tile, preferred_element_type=jnp.float32
                    ),
                    jnp.einsum(
                        "hid,jd->hij", upstream_tile, value_tile, preferred_element_type=jnp.float32
                    ),
                )

            def empty_pair():
                return (
                    jnp.zeros((head_count, tile_rows, head_size), jnp.float32),
                    jnp.zeros((head_count, tile_rows, tile_rows), jnp.float32),
                )

            contribution, prob_grad_tile = lax.cond(active[column_index], forward_tile, empty_pair)
            attended = attended + contribution
            grad_tiles.append(prob_grad_tile)
        prob_grad = jnp.concatenate(grad_tiles, axis=-1)
        row_delta = jnp.sum(probability * prob_grad, axis=-1, keepdims=True)
        score_grad = (probability * (prob_grad - row_delta) * softmax_scale).astype(jnp.bfloat16)
        query_sum = jnp.zeros((head_count, tile_rows, head_size), jnp.float32)
        for column_index in range(block_index + 1):
            column_start = column_index * tile_rows
            key_tile = key_rows[column_start : column_start + tile_rows]
            score_piece = score_grad[:, :, column_start : column_start + tile_rows]
            weight_tile = weights[:, :, column_start : column_start + tile_rows]

            def backward_tile(
                score_piece=score_piece,
                key_tile=key_tile,
                weight_tile=weight_tile,
                query_tile=query_tile,
                upstream_tile=upstream_tile,
            ):
                return (
                    jnp.einsum(
                        "hij,jd->hid", score_piece, key_tile, preferred_element_type=jnp.float32
                    ),
                    jnp.einsum(
                        "hij,hid->jd", score_piece, query_tile, preferred_element_type=jnp.float32
                    ),
                    jnp.einsum(
                        "hij,hid->jd",
                        weight_tile,
                        upstream_tile,
                        preferred_element_type=jnp.float32,
                    ),
                )

            def empty_triple():
                return (
                    jnp.zeros((head_count, tile_rows, head_size), jnp.float32),
                    empty_rows,
                    empty_rows,
                )

            query_part, key_part, value_part = lax.cond(
                active[column_index], backward_tile, empty_triple
            )
            query_sum = query_sum + query_part
            key_sums[column_index] = key_sums[column_index] + key_part
            value_sums[column_index] = value_sums[column_index] + value_part
        attended_blocks.append(attended.astype(jnp.bfloat16))
        grad_blocks.append(query_sum.astype(jnp.bfloat16))
    return (
        jnp.concatenate(attended_blocks, axis=1),
        jnp.concatenate(grad_blocks, axis=1),
        jnp.concatenate(key_sums, axis=0),
        jnp.concatenate(value_sums, axis=0),
    )


def grad_term(grad_full, attended_heads):
    attended_flat = from_heads(attended_heads)
    return lax.dot_general(
        grad_full, attended_flat, (((0,), (0,)), ((), ())), preferred_element_type=jnp.float32
    )


def per_device(query_rows, key_rows, value_matrix, out_weight, out_grad, doc_lengths):
    row_count = query_rows.shape[0]
    weight_full = lax.all_gather(out_weight, "dp", axis=1, tiled=True)
    grad_full = collect(out_grad, "mp", 1)
    attn_grad = lax.dot_general(
        grad_full, weight_full, (((1,), (1,)), ((), ())), preferred_element_type=jnp.float32
    ).astype(jnp.bfloat16)
    segment = local_segments(doc_lengths[0], row_count)
    queries = to_heads(query_rows)
    upstreams = to_heads(attn_grad)
    attended, query_grad, key_sum, value_sum = attend(
        queries, key_rows, value_matrix, upstreams, segment
    )
    key_grad = key_sum.astype(jnp.bfloat16)
    value_grad = value_sum.astype(jnp.bfloat16)
    weight_part = lax.psum_scatter(
        grad_term(grad_full, attended).astype(jnp.bfloat16), "dp", scatter_dimension=0, tiled=True
    ).astype(jnp.float32)
    attended_flat = from_heads(attended)
    query_grad = from_heads(query_grad)
    partial_sum = jnp.dot(attended_flat, weight_full, preferred_element_type=jnp.float32).astype(
        jnp.bfloat16
    )
    layer_out = sum_at_owner(
        lax.optimization_barrier(partial_sum).astype(jnp.float32).astype(jnp.bfloat16), "mp", 1
    ).astype(jnp.bfloat16)
    return (layer_out, query_grad, key_grad, value_grad, weight_part.T)


def solution(mesh):
    placed = (
        P("dp", "mp"),
        P("dp", "mp"),
        P("dp", "mp"),
        P("mp", "dp"),
        P("dp", "mp"),
        P("dp", None),
    )
    return jax.shard_map(
        per_device,
        mesh=mesh,
        in_specs=placed,
        out_specs=(P("dp", "mp"), P("dp", "mp"), P("dp", "mp"), P("dp", "mp"), P("mp", "dp")),
        check_vma=False,
    )
```

profile of v0, /device:TPU:8, one launch (start us, length us, event | category | flops | bytes accessed | tf_op | source)
XLA Modules:
  0.0 271.5 jit_solution(7485952479095760482)
XLA Ops:
  7.2 0.7 all-gather.2.cloned.1.call-update
  7.9 1.3 copy.94
  9.3 1.6 broadcast_in_dim.40
  10.9 5.9 %all-to-all-start = ((bf16[4,256,1280]{1,2,0:T(8,128)(2,1)}), bf16[4,256,1280]{1,2,0:T(8,128)(2,1)S(1)}, u32[]{:S(2)}, u32[]{:S(2)}) async-start(bf16[4,256,1280]{1,2,0:T(8,128)(2,1)} %broadcast_in_dim.40), calls=%async_computation | async-start | bytes 5242880 | tf_op jit(solution)/shard_map/all_to_all | solution.py:12
  20.5 0.6 fusion.67
  21.2 1.1 conditional.9
  21.3 1.0 fusion
  22.3 0.9 copy.98
  23.4 1.1 conditional.11
  23.5 1.0 fusion.5
  24.6 0.8 copy.102
  26.8 1.1 conditional.12
  26.9 1.0 fusion.7
  28.2 0.6 slice.74
  28.8 2.0 fusion.62
  30.8 1.8 fusion.70
  32.7 13.8 %all-to-all-done = bf16[4,256,1280]{1,2,0:T(8,128)(2,1)S(1)} async-done(((bf16[4,256,1280]{1,2,0:T(8,128)(2,1)}), bf16[4,256,1280]{1,2,0:T(8,128)(2,1)S(1)}, u32[]{:S(2)}, u32[]{:S(2)}) %all-to-all-start) | async-done | bytes 2621472 | tf_op jit(solution)/shard_map/all_to_all | solution.py:12
  46.4 46.9 %all-gather.2.cloned.1.call-done = bf16[512,5120]{0,1:T(8,128)(2,1)} async-done(((bf16[512,80]{0,1:T(8,128)(2,1)}), bf16[512,5120]{0,1:T(8,128)(2,1)}) %all-gather.2.cloned.1.call-update) | async-done | bytes 5242896 | tf_op jit(solution)/shard_map/all_gather | solution.py:193
  93.3 4.1 %fusion.42 = bf16[32,4,8,128]{3,2,1,0:T(8,128)(2,1)S(1)} fusion(bf16[256,5120]{0,1:T(8,128)(2,1)S(1)} %bitcast.117, bf16[512,5120]{0,1:T(8,128)(2,1)} %all-gather.2.cloned.1.call-done), kind=kOutput, calls=%fused_computation.61 | convolution fusion | flops 1342308352 | bytes 8126464 | tf_op jit(solution)/shard_map/dot_general | solution.py:195
  97.4 0.7 fusion.65
  98.1 2.7 conditional.10
  98.1 0.6 copy-done.8
  98.9 0.8 copy.137
  99.7 1.1 fusion.3
  100.8 2.0 conditional.13
  100.8 1.0 fusion.9
  101.8 1.0 fusion.11
  102.8 0.7 copy-done.2
  103.6 1.9 conditional.14
  103.6 0.9 fusion.13
  104.5 1.0 fusion.15
  105.5 1.1 add_convert_fusion.1
  106.6 0.9 pad_maximum_fusion
  107.6 3.9 %fusion.33 = bf16[5120,512]{0,1:T(8,128)(2,1)} fusion(bf16[256,512]{0,1:T(8,128)(2,1)S(1)} %bitcast.121, bf16[256,5120]{0,1:T(8,128)(2,1)S(1)} %bitcast.118), kind=kOutput, calls=%fused_computation.49 | convolution fusion | flops 1344798720 | bytes 8126464 | tf_op jit(solution)/shard_map/dot_general | solution.py:186
  111.5 7.9 %copy.134 = bf16[5120,512]{1,0:T(8,128)(2,1)} copy(bf16[5120,512]{0,1:T(8,128)(2,1)} %fusion.33) | data formatting | bytes 10485760
  119.5 4.1 %convolution_convert_fusion.3 = bf16[256,5120]{1,0:T(8,128)(2,1)S(1)} fusion(bf16[256,512]{0,1:T(8,128)(2,1)S(1)} %bitcast.122, bf16[512,5120]{0,1:T(8,128)(2,1)} %all-gather.2.cloned.1.call-done), kind=kOutput, calls=%fused_computation.50 | convolution fusion | flops 1343488000 | bytes 8126464 | tf_op jit(solution)/shard_map/dot_general | solution.py:211
  123.6 1.7 copy.154
  125.2 4.8 %all-to-all-start.1 = ((bf16[4,256,1280]{2,1,0:T(8,128)(2,1)}), bf16[4,256,1280]{2,1,0:T(8,128)(2,1)S(1)}, u32[]{:S(2)}, u32[]{:S(2)}) async-start(bf16[4,256,1280]{2,1,0:T(8,128)(2,1)} %bitcast.119), calls=%async_computation.1 | async-start | bytes 5242880 | tf_op jit(solution)/shard_map/all_to_all | solution.py:34
  130.1 1.0 constant_dynamic-update-slice_fusion
  131.0 1.4 fusion.37
  132.4 1.3 fusion.43
  133.7 2.3 conditional.15
  133.7 1.1 convolution_bitcast_fusion
  135.1 1.0 convolution_convert_fusion.1
  136.1 0.6 copy-done.10
  136.8 3.8 %conditional.17 = (f32[4,128,128]{2,1,0:T(8,128)S(1)}, bf16[128,128]{1,0:T(8,128)(2,1)S(1)}, bf16[128,128]{1,0:T(8,128)(2,1)}) conditional(s32[]{:T(128)} %bitcast.26, () %tuple.94, (bf16[4,128,256]{1,2,0:T(8,128)(2,1)S(1)}, bf16[128,128]{1,0:T(8,128)(2,1)}, bf16[4,128,128]{1,2,0:T(8,128)(2,1)S(1)}, bf16[4,128,128]{1,2,0:T(8,128)(2,1)}, ...), branch_computations={%region_26.27_spmd, %region_27.28_spmd} | conditional | flops 50364416 | bytes 2588724 | solution.py:168
  136.8 1.7 fusion.25
  138.6 0.7 copy-done.6
  139.5 1.1 fusion.27
  141.2 3.9 %conditional.16 = (f32[4,128,128]{2,1,0:T(8,128)S(1)}, f32[128,128]{1,0:T(8,128)S(1)}, f32[128,128]{1,0:T(8,128)}) conditional(s32[]{:T(128)} %bitcast.24, () %tuple.92, (bf16[4,128,256]{1,2,0:T(8,128)(2,1)S(1)}, bf16[128,128]{1,0:T(8,128)(2,1)}, bf16[4,128,128]{1,2,0:T(8,128)(2,1)S(1)}, bf16[4,128,128]{1,2,0:T(8,128)(2,1)S(1)}, ...), branch_computations={%region_24.25_spmd, %region_25.26_spmd} | conditional | flops 50331648 | bytes 1605656 | solution.py:168
  141.2 0.8 convolution_bitcast_fusion.2
  142.0 0.8 copy.116
  142.9 1.1 convolution_bitcast_fusion.3
  144.0 1.1 fusion.21
  145.1 0.9 add_convert_fusion.2
  146.0 1.4 pad_maximum_fusion.2
  147.4 0.9 add_convert_fusion.3
  148.2 1.4 pad_maximum_fusion.1
  149.7 1.7 copy_bitcast_fusion
  151.3 9.6 %all-to-all-done.1 = bf16[4,256,1280]{2,1,0:T(8,128)(2,1)S(1)} async-done(((bf16[4,256,1280]{2,1,0:T(8,128)(2,1)}), bf16[4,256,1280]{2,1,0:T(8,128)(2,1)S(1)}, u32[]{:S(2)}, u32[]{:S(2)}) %all-to-all-start.1) | async-done | bytes 2621472 | tf_op jit(solution)/shard_map/all_to_all | solution.py:34
  160.9 1.4 reduce_sum.60
  162.3 100.5 %reduce-scatter.4.cloned.1.call-done = bf16[80,512]{1,0:T(8,128)(2,1)} async-done(((bf16[5120,512]{1,0:T(8,128)(2,1)}), bf16[80,512]{1,0:T(8,128)(2,1)}) %reduce-scatter.4.cloned.1.call-update) | async-done | bytes 81936
  262.8 1.0 copy.135
  263.9 0.8 copy.121
  (65 shorter events, 3.7 us)
Async XLA Ops:
  7.2 9.7 %copy-start.17 = (s32[1,8]{1,0:T(1,128)S(1)}, s32[1,8]{1,0:T(1,128)}, u32[]{:S(2)}) copy-start(s32[1,8]{1,0:T(1,128)} %param.29) | copy-start | bytes 100
  7.2 13.1 %copy-start.11 = (bf16[256,512]{1,0:T(8,128)(2,1)S(1)}, bf16[256,512]{1,0:T(8,128)(2,1)}, u32[]{:S(2)}) copy-start(bf16[256,512]{1,0:T(8,128)(2,1)} %param.24) | copy-start | bytes 786436
  7.2 13.3 %copy-start.16 = (bf16[256,128]{1,0:T(8,128)(2,1)S(1)}, bf16[256,128]{1,0:T(8,128)(2,1)}, u32[]{:S(2)}) copy-start(bf16[256,128]{1,0:T(8,128)(2,1)} %param.25) | copy-start | bytes 196612
  7.2 86.1 %all-gather.2.cloned.1.call-start = ((), (), s32[]{:S(2)}) async-start(), calls=%async_computation.3 | async-start | bytes 5324800 | tf_op jit(solution)/shard_map/all_gather | solution.py:193
  10.9 17.3 %copy-start.14 = (bf16[256,128]{1,0:T(8,128)(2,1)S(1)}, bf16[256,128]{1,0:T(8,128)(2,1)}, u32[]{:S(2)}) copy-start(bf16[256,128]{1,0:T(8,128)(2,1)} %param.26) | copy-start | bytes 196612
  10.9 35.5 %all-to-all-start = ((bf16[4,256,1280]{1,2,0:T(8,128)(2,1)}), bf16[4,256,1280]{1,2,0:T(8,128)(2,1)S(1)}, u32[]{:S(2)}, u32[]{:S(2)}) async-start(bf16[4,256,1280]{1,2,0:T(8,128)(2,1)} %broadcast_in_dim.40), calls=%async_computation | async-start | bytes 5242880 | tf_op jit(solution)/shard_map/all_to_all | solution.py:12
  16.8 246.0 %reduce-scatter.4.cloned.1.call-start = ((), (), s32[]{:S(2)}) async-start(), calls=%async_computation.4 | async-start | bytes 5324800
  30.8 72.0 %copy-start = (bf16[4,128,128]{1,2,0:T(8,128)(2,1)}, bf16[4,128,128]{1,2,0:T(8,128)(2,1)S(1)}, u32[]{:S(2)}) copy-start(bf16[4,128,128]{1,2,0:T(8,128)(2,1)S(1)} %get-tuple-element.377) | copy-start | bytes 393220
  93.3 4.8 %copy-start.7 = (bf16[128,128]{1,0:T(8,128)(2,1)S(1)}, bf16[128,128]{1,0:T(8,128)(2,1)}, u32[]{:S(2)}) copy-start(bf16[128,128]{1,0:T(8,128)(2,1)} %slice.74) | copy-start | bytes 98308
  93.3 4.8 %copy-start.9 = (bf16[4,128,128]{1,2,0:T(8,128)(2,1)S(1)}, bf16[4,128,128]{1,2,0:T(8,128)(2,1)}, u32[]{:S(2)}) copy-start(bf16[4,128,128]{1,2,0:T(8,128)(2,1)} %get-tuple-element.387) | copy-start | bytes 393220
  98.1 0.6 copy-start.8
  100.8 5.8 %copy-start.1 = (f32[4,128,128]{1,2,0:T(8,128)}, f32[4,128,128]{1,2,0:T(8,128)S(1)}, u32[]{:S(2)}) copy-start(f32[4,128,128]{1,2,0:T(8,128)S(1)} %get-tuple-element.366) | copy-start | bytes 786436
  102.8 0.7 copy-start.2
  102.8 0.8 copy-start.4
  105.5 1.1 copy-start.5
  123.5 6.5 %copy-start.3 = (f32[4,128,128]{1,2,0:T(8,128)S(1)}, f32[4,128,128]{1,2,0:T(8,128)}, u32[]{:S(2)}) copy-start(f32[4,128,128]{1,2,0:T(8,128)} %copy-done.2) | copy-start | bytes 786436
  125.2 35.7 %all-to-all-start.1 = ((bf16[4,256,1280]{2,1,0:T(8,128)(2,1)}), bf16[4,256,1280]{2,1,0:T(8,128)(2,1)S(1)}, u32[]{:S(2)}, u32[]{:S(2)}) async-start(bf16[4,256,1280]{2,1,0:T(8,128)(2,1)} %bitcast.119), calls=%async_computation.1 | async-start | bytes 5242880 | tf_op jit(solution)/shard_map/all_to_all | solution.py:34
  136.1 0.7 copy-start.10
  136.1 0.7 copy-start.12
  136.1 0.7 copy-start.13
  138.6 0.7 copy-start.6
  140.6 0.6 copy-start.15
Sparse Core Ops, SparseCore 0:
  10.8 82.4 all-gather.1
  119.6 143.1 reduce-scatter.3
where the time goes:
time: 273 us; the launch traced here: 271 us
  waiting for transfers between devices  171 us (63%)
  matrix products  28.4 us (10%)
  local copies, waits for them, and re-layouts  25.2 us (9%)
  between operations  18.3 us (7%)
  other arithmetic  17.1 us (6%)
  starting transfers between devices  10.8 us (4%)
    unnamed x3, waiting for transfers between devices  101 us
    all_gather x1, waiting for transfers between devices, per_device(): weight_full = lax.all_gather(out_weight, 'dp', axis=1, tiled=True)  46.9 us
    all_to_all x1, waiting for transfers between devices, from_everyone(): lax.all_to_all(jnp.broadcast_to(x[None], (size, *x.shape)), axis, 0, 0, t...  13.8 us
    unnamed x38, local copies, waits for them, and re-layouts  13.3 us
    all_to_all x1, waiting for transfers between devices, sum_at_owner(): lax.all_to_all(pieces, axis, split_axis=0, concat_axis=0, tiled=True)  9.61 us
    all_to_all x1, starting transfers between devices, from_everyone(): lax.all_to_all(jnp.broadcast_to(x[None], (size, *x.shape)), axis, 0, 0, t...  5.91 us
  transfers between devices with their start and end apart: 4, of which 4 were waited for; matrix products, arithmetic and copies ran while one was open for 15% of the time, Pallas kernels for 0%

commit v1 on v0

v1 whole, which is shorter than its diff:
```python
import functools

import jax
import jax.numpy as jnp
from jax import lax
from jax.experimental import pallas as pl
from jax.experimental.pallas import tpu as pltpu
from jax.sharding import PartitionSpec as P

NX, NZ, NC, NY = 4, 8, 2, 4
HEAD = 128
TOK = 256
HEADS = 4
GROUP = HEADS * HEAD
COLS = 1280
SHARD = 80
FIRST = 32
REST = SHARD - FIRST
AXES = ("dp", "mp")
BF, F32 = jnp.bfloat16, jnp.float32
SCALE = HEAD ** -0.5


def route(target):
    pairs = []
    for x in range(NX):
        for z in range(NZ):
            for c in range(NC):
                for y in range(NY):
                    tx, tz, tc, ty = target(x, z, c, y)
                    src = ((x * NZ + z) * NC + c) * NY + y
                    pairs.append((src, ((tx * NZ + tz) * NC + tc) * NY + ty))
    return pairs


SWAP = route(lambda x, z, c, y: (x, z, 1 - c, y))
TO_PLANE = [route(lambda x, z, c, y, k=k: ((2 * (y % 2) + c + k) % 4, z, y // 2, x)) for k in range(4)]
TO_OWNER = [
    route(lambda x, z, c, y, k=k: (y, z, (x + k) % 4 % 2, 2 * c + (x + k) % 4 // 2)) for k in range(4)
]
HEADS_OUT = [route(lambda x, z, c, y, k=k: (x, z, y // 2, (2 * (y % 2) + c + k) % 4)) for k in range(4)]
HEADS_BACK = [
    route(lambda x, z, c, y, k=k: (x, z, (y + k) % 4 % 2, 2 * c + (y + k) % 4 // 2)) for k in range(4)
]
Z_GROUPS = [[(x * NZ + z) * NC + c for z in range(NZ)] for x in range(NX) for c in range(NC)]


def send(value, pairs):
    return lax.ppermute(value, AXES, pairs)


def over_z(blocks):
    return lax.all_to_all(blocks, "dp", 0, 0, axis_index_groups=Z_GROUPS, tiled=True)


def dot(a, b, dims):
    return lax.dot_general(a, b, (dims, ((), ())), preferred_element_type=F32)


def call(body, outs, scratch=(), flops=0, moved=0, prefetch=1, name=None):
    def run(scalars, *operands):
        vmem = pl.BlockSpec(memory_space=pltpu.VMEM)
        return pl.pallas_call(
            body,
            out_shape=outs,
            in_specs=[pl.BlockSpec(memory_space=pltpu.SMEM)] + [vmem] * len(operands),
            out_specs=jax.tree.map(lambda _: vmem, outs),
            scratch_shapes=list(scratch),
            compiler_params=pltpu.CompilerParams(vmem_limit_bytes=40 << 20),
            cost_estimate=pl.CostEstimate(flops=flops, bytes_accessed=moved, transcendentals=0),
            name=name,
        )(scalars, *operands)

    return run


def shape(*dims, dtype=BF):
    return jax.ShapeDtypeStruct(dims, dtype)


def forward_body(lengths, q_ref, k_ref, v_ref, att_ref, prob_ref):
    rows = lax.broadcasted_iota(jnp.int32, (TOK, TOK), 0)
    cols = lax.broadcasted_iota(jnp.int32, (TOK, TOK), 1)
    row_at = lax.broadcasted_iota(jnp.int32, (TOK, 1), 0)
    col_at = lax.broadcasted_iota(jnp.int32, (1, TOK), 1)
    row_seg = jnp.zeros((TOK, 1), jnp.int32)
    col_seg = jnp.zeros((1, TOK), jnp.int32)
    end = jnp.int32(0)
    for i in range(8):
        end = end + lengths[i]
        row_seg = row_seg + (row_at >= end).astype(jnp.int32)
        col_seg = col_seg + (col_at >= end).astype(jnp.int32)
    allowed = (row_seg == col_seg) & (rows >= cols)
    for h in range(HEADS):
        at = slice(h * HEAD, (h + 1) * HEAD)
        logits = dot(q_ref[:, at], k_ref[...], ((1,), (1,))) * SCALE
        logits = jnp.where(allowed, logits, -jnp.inf)
        terms = jnp.exp(logits - jnp.max(logits, axis=-1, keepdims=True))
        prob = terms / jnp.sum(terms, axis=-1, keepdims=True)
        prob_ref[h] = prob
        att_ref[:, at] = dot(prob.astype(BF), v_ref[...], ((1,), (0,))).astype(BF)


def backward_body(_, a0, a1, a2, a3, q_ref, k_ref, v_ref, prob_ref, dq_ref, dk_ref, dv_ref):
    key_sum = jnp.zeros((TOK, HEAD), F32)
    value_sum = jnp.zeros((TOK, HEAD), F32)
    for h in range(HEADS):
        at = slice(h * HEAD, (h + 1) * HEAD)
        up = (
            (a0[:, at].astype(F32) + a1[:, at].astype(F32))
            + (a2[:, at].astype(F32) + a3[:, at].astype(F32))
        ).astype(BF)
        prob = prob_ref[h]
        prob_grad = dot(up, v_ref[...], ((1,), (1,)))
        delta = jnp.sum(prob * prob_grad, axis=-1, keepdims=True)
        score = (prob * (prob_grad - delta) * SCALE).astype(BF)
        dq_ref[:, at] = dot(score, k_ref[...], ((1,), (0,))).astype(BF)
        key_sum = key_sum + dot(score, q_ref[:, at], ((0,), (0,)))
        value_sum = value_sum + dot(prob.astype(BF), up, ((0,), (0,)))
    dk_ref[...] = key_sum.astype(BF)
    dv_ref[...] = value_sum.astype(BF)


def weight_grad_body(place, own, other, r0, r1, r2, r3, first_ref, b0, b1, b2, b3, att_ref, og, total):
    x, c, y = place[0], place[1], place[2]
    og[pl.ds(pl.multiple_of(c * TOK, TOK), TOK), :] = own[...]
    og[pl.ds(pl.multiple_of((1 - c) * TOK, TOK), TOK), :] = other[...]
    for k, ref in enumerate((r0, r1, r2, r3)):
        j = (y + 4 - k) % 4
        att_ref[
            pl.ds(pl.multiple_of((j % 2) * TOK, TOK), TOK),
            pl.ds(pl.multiple_of((j // 2) * GROUP, GROUP), GROUP),
        ] = ref[...]
    for i in range(COLS // 256):
        total[i * 256 : (i + 1) * 256, :] = dot(
            og[:, i * 256 : (i + 1) * 256], att_ref[...], ((0,), (0,))
        ).astype(BF)
    for z in range(NZ):
        for j in range(4):
            first_ref[z, j * FIRST : (j + 1) * FIRST, :] = total[
                z * 160 + (j % 2) * SHARD : z * 160 + (j % 2) * SHARD + FIRST,
                (j // 2) * GROUP : (j // 2 + 1) * GROUP,
            ]
    for k, ref in enumerate((b0, b1, b2, b3)):
        j = (x + k) % 4
        for z in range(NZ):
            ref[z] = total[
                pl.ds(pl.multiple_of(z * 160 + (j % 2) * SHARD + FIRST, 16), REST),
                pl.ds(pl.multiple_of((j // 2) * GROUP, GROUP), GROUP),
            ]


def attn_grad_body(place, own, other, first, w0, w1, w2, w3, g0, g1, g2, g3, wt_ref, og):
    x, c, y = place[0], place[1], place[2]
    og[pl.ds(pl.multiple_of(c * TOK, TOK), TOK), :] = own[...]
    og[pl.ds(pl.multiple_of((1 - c) * TOK, TOK), TOK), :] = other[...]
    for k, ref in enumerate((w0, w1, w2, w3)):
        j = (x + 4 - k) % 4
        lanes = pl.ds(pl.multiple_of((j // 2) * GROUP, GROUP), GROUP)
        for z in range(NZ):
            base = z * 160 + (j % 2) * SHARD
            wt_ref[pl.ds(pl.multiple_of(base, 16), FIRST), lanes] = first[z, k * FIRST : (k + 1) * FIRST, :]
            wt_ref[pl.ds(pl.multiple_of(base + FIRST, 16), REST), lanes] = ref[z]
    for k, ref in enumerate((g0, g1, g2, g3)):
        m = (y + k) % 4
        ref[...] = dot(
            og[pl.ds(pl.multiple_of((m % 2) * TOK, TOK), TOK), :],
            wt_ref[:, pl.ds(pl.multiple_of((m // 2) * GROUP, GROUP), GROUP)],
            ((1,), (0,)),
        ).astype(BF)


def layer_out_body(place, att, wt, mine_ref, theirs_ref):
    c = place[1]
    mine_ref[...] = dot(att[pl.ds(pl.multiple_of(c * TOK, TOK), TOK), :], wt[...], ((1,), (1,)))
    theirs_ref[...] = dot(
        att[pl.ds(pl.multiple_of((1 - c) * TOK, TOK), TOK), :], wt[...], ((1,), (1,))
    ).astype(BF)


def sum_four_body(_, b0, b1, b2, b3, out):
    for z in range(NZ):
        out[z] = (
            (b0[z].astype(F32) + b1[z].astype(F32)) + (b2[z].astype(F32) + b3[z].astype(F32))
        ).astype(BF)


def sum_z_body(place, blocks, o0, o1, o2, o3):
    x = place[0]
    for k, ref in enumerate((o0, o1, o2, o3)):
        j = (x + k) % 4
        at = pl.ds(pl.multiple_of(j * FIRST, FIRST), FIRST)
        total = blocks[0, at, :].astype(F32)
        for z in range(1, NZ):
            total = total + blocks[z, at, :].astype(F32)
        ref[...] = total.astype(BF)


def finish_body(_, o0, o1, o2, o3, blocks, out):
    out[:FIRST, :] = (o0[...].astype(F32) + o1[...].astype(F32)) + (
        o2[...].astype(F32) + o3[...].astype(F32)
    )
    total = blocks[0].astype(F32)
    for z in range(1, NZ):
        total = total + blocks[z].astype(F32)
    out[FIRST:, :] = total


def per_device(query_rows, key_rows, value_matrix, out_weight, out_grad, doc_lengths):
    dp, y = lax.axis_index("dp"), lax.axis_index("mp")
    place = jnp.stack([dp // (NZ * NC), dp % NC, y]).astype(jnp.int32)
    wt = out_weight.T
    first_xy = [send(wt[:FIRST], pairs) for pairs in TO_PLANE]
    rest_z = over_z(jnp.broadcast_to(wt[FIRST:][None], (NZ, REST, GROUP)))
    other_grad = send(out_grad, SWAP)

    attended, prob = call(
        forward_body,
        (shape(TOK, GROUP), shape(HEADS, TOK, TOK, dtype=F32)),
        flops=4 * 4 * TOK * TOK * HEAD,
        moved=2 << 20,
        name="attention_forward",
    )(doc_lengths[0], query_rows, key_rows, value_matrix)
    heads = [send(attended, pairs) for pairs in HEADS_OUT]

    first_w = over_z(jnp.broadcast_to(jnp.concatenate(first_xy, axis=0)[None], (NZ, 4 * FIRST, GROUP)))
    rest_w = [send(rest_z, pairs) for pairs in TO_PLANE]

    big = 2 * 2 * TOK * COLS * 2 * GROUP
    grads = call(
        weight_grad_body,
        (shape(NZ, 4 * FIRST, GROUP),)
        + (shape(NZ, REST, GROUP),) * 4
        + (shape(2 * TOK, 2 * GROUP),),
        scratch=(pltpu.VMEM((2 * TOK, COLS), BF), pltpu.VMEM((COLS, 2 * GROUP), BF)),
        flops=big,
        moved=8 << 20,
        name="weight_grad",
    )(place, out_grad, other_grad, *heads)
    first_part, rest_parts, attended_two = grads[0], grads[1:5], grads[5]

    *partials, wt_two = call(
        attn_grad_body,
        (shape(TOK, GROUP),) * 4 + (shape(COLS, 2 * GROUP),),
        scratch=(pltpu.VMEM((2 * TOK, COLS), BF),),
        flops=big,
        moved=8 << 20,
        name="attn_grad",
    )(place, out_grad, other_grad, first_w, *rest_w)
    upstream = [send(partial, pairs) for partial, pairs in zip(partials, HEADS_BACK)]

    mine, theirs = call(
        layer_out_body,
        (shape(TOK, COLS, dtype=F32), shape(TOK, COLS)),
        flops=big,
        moved=6 << 20,
        name="layer_out",
    )(place, attended_two, wt_two)
    layer_out = (mine + send(theirs, SWAP).astype(F32)).astype(BF)

    rest_xy = [send(part, pairs) for part, pairs in zip(rest_parts, TO_OWNER)]
    first_sum = over_z(first_part)
    rest_sum = call(sum_four_body, shape(NZ, REST, GROUP), moved=2 << 20, name="sum_four")(
        place, *rest_xy
    )
    rest_sum = over_z(rest_sum)
    pieces = call(sum_z_body, (shape(FIRST, GROUP),) * 4, moved=1 << 20, name="sum_z")(place, first_sum)
    pieces = [send(piece, pairs) for piece, pairs in zip(pieces, TO_OWNER)]
    weight_grad = call(finish_body, shape(SHARD, GROUP, dtype=F32), moved=1 << 20, name="finish")(
        place, *pieces, rest_sum
    )

    query_grad, key_grad, value_grad = call(
        backward_body,
        (shape(TOK, GROUP), shape(TOK, HEAD), shape(TOK, HEAD)),
        flops=5 * 4 * 2 * TOK * TOK * HEAD,
        moved=3 << 20,
        name="attention_backward",
    )(place, *upstream, query_rows, key_rows, value_matrix, prob)
    return (layer_out, query_grad, key_grad, value_grad, weight_grad.T)


def solution(mesh):
    placed = (
        P("dp", "mp"),
        P("dp", "mp"),
        P("dp", "mp"),
        P("mp", "dp"),
        P("dp", "mp"),
        P("dp", None),
    )
    return jax.shard_map(
        per_device,
        mesh=mesh,
        in_specs=placed,
        out_specs=(P("dp", "mp"), P("dp", "mp"), P("dp", "mp"), P("dp", "mp"), P("mp", "dp")),
        check_vma=False,
    )
```

time: 273 us -> 214 us (0.78)
  the two profiles are of different devices: /device:TPU:8 before, /device:TPU:15 now
where the time goes in v1:
time: 214 us; the launch traced here: 213 us
  starting transfers between devices  110 us (51%)
  waiting for transfers between devices  71 us (33%)
  Pallas kernels  19.3 us (9%)
  local copies, waits for them, and re-layouts  10 us (5%)
    ppermute x26, starting transfers between devices, send(): return lax.ppermute(value, AXES, pairs)  81.1 us
    ppermute x26, waiting for transfers between devices, send(): return lax.ppermute(value, AXES, pairs)  71 us
    all_to_all x4, starting transfers between devices, over_z(): lax.all_to_all(blocks, 'dp', 0, 0, axis_index_groups=Z_GROUPS, tiled=True)  28.4 us
    pallas_call x8, Pallas kernels, run(): pl.pallas_call(body, out_shape=outs, in_specs=[pl.BlockSpec(memory_space=...  19.3 us
    unnamed x28, local copies, waits for them, and re-layouts  6.56 us
  transfers between devices with their start and end apart: 30, of which 12 were waited for; matrix products, arithmetic and copies ran while one was open for 1% of the time, Pallas kernels for 8%

profile of v1, /device:TPU:15, one launch (start us, length us, event | category | flops | bytes accessed | tf_op | source)
XLA Modules:
  0.0 213.0 jit_solution(12619754889300754944)
XLA Ops:
  0.6 0.8 slice.12
  1.4 0.8 broadcast_in_dim.5
  2.2 8.2 %all-to-all-start.1 = ((bf16[8,48,512]{2,1,0:T(8,128)(2,1)}), bf16[8,48,512]{2,1,0:T(8,128)(2,1)}, u32[]{:S(2)}, u32[]{:S(2)}) async-start(bf16[8,48,512]{2,1,0:T(8,128)(2,1)} %broadcast_in_dim.5), calls=%async_computation.1 | async-start | bytes 786432 | tf_op jit(solution)/shard_map/all_to_all | solution.py:53
  10.4 0.8 slice.11
  11.2 5.0 %collective-permute-start.8 = (bf16[32,512]{1,0:T(8,128)(2,1)S(1)}, bf16[32,512]{1,0:T(8,128)(2,1)S(1)}, u32[]{:S(2)}, u32[]{:S(2)}) collective-permute-start(bf16[32,512]{1,0:T(8,128)(2,1)S(1)} %slice.11), channel_id=1, source_target_pairs={{0,192},{1,64},{2,196},{3,68},{4,0},{5,128},{6,4},{7,132},{8,200},... | collective-permute-start | bytes 98312 | tf_op jit(solution)/shard_map/ppermute | solution.py:49
  16.2 1.1 collective-permute-start.7
  17.2 1.9 collective-permute-start.6
  19.2 3.2 %collective-permute-start.5 = (bf16[32,512]{1,0:T(8,128)(2,1)S(1)}, bf16[32,512]{1,0:T(8,128)(2,1)S(1)}, u32[]{:S(2)}, u32[]{:S(2)}) collective-permute-start(bf16[32,512]{1,0:T(8,128)(2,1)S(1)} %slice.11), channel_id=1, source_target_pairs={{0,0},{1,128},{2,4},{3,132},{4,64},{5,192},{6,68},{7,196},{8,8},{9... | collective-permute-start | bytes 98312 | tf_op jit(solution)/shard_map/ppermute | solution.py:49
  22.4 0.0 collective-permute-done.8
  22.4 0.0 collective-permute-done.7
  22.4 4.0 %collective-permute-done.6 = bf16[32,512]{1,0:T(8,128)(2,1)S(1)} collective-permute-done((bf16[32,512]{1,0:T(8,128)(2,1)S(1)}, bf16[32,512]{1,0:T(8,128)(2,1)S(1)}, u32[]{:S(2)}, u32[]{:S(2)}) %collective-permute-start.6) | collective-permute-done | bytes 32800 | tf_op jit(solution)/shard_map/ppermute | solution.py:49
  26.4 1.3 collective-permute-done.5
  27.8 1.1 broadcast_in_dim.4
  28.9 0.0 copy-start.11
  28.9 6.8 %all-to-all-start = ((bf16[8,128,512]{2,1,0:T(8,128)(2,1)}), bf16[8,128,512]{2,1,0:T(8,128)(2,1)S(1)}, u32[]{:S(2)}, u32[]{:S(2)}) async-start(bf16[8,128,512]{2,1,0:T(8,128)(2,1)} %broadcast_in_dim.4), calls=%async_computation | async-start | bytes 2097152 | tf_op jit(solution)/shard_map/all_to_all | solution.py:53
  35.7 0.1 collective-permute-start
  35.8 1.7 attention_forward.1
  37.5 1.0 copy-done
  38.5 3.0 %collective-permute-start.4 = (bf16[256,512]{1,0:T(8,128)(2,1)S(1)}, bf16[256,512]{1,0:T(8,128)(2,1)S(1)}, u32[]{:S(2)}, u32[]{:S(2)}) collective-permute-start(bf16[256,512]{1,0:T(8,128)(2,1)S(1)} %get-tuple-element.27), channel_id=1, source_target_pairs={{0,3},{1,1},{2,7},{3,5},{4,0},{5,2},{6,4},{7,6},{8,11},{9,9},{10,1... | collective-permute-start | bytes 786440 | tf_op jit(solution)/shard_map/ppermute | solution.py:49
  41.5 0.1 collective-permute-start.3
  41.6 4.7 %collective-permute-start.2 = (bf16[256,512]{1,0:T(8,128)(2,1)S(1)}, bf16[256,512]{1,0:T(8,128)(2,1)S(1)}, u32[]{:S(2)}, u32[]{:S(2)}) collective-permute-start(bf16[256,512]{1,0:T(8,128)(2,1)S(1)} %get-tuple-element.27), channel_id=1, source_target_pairs={{0,1},{1,3},{2,5},{3,7},{4,2},{5,0},{6,6},{7,4},{8,9},{9,11},{10,1... | collective-permute-start | bytes 786440 | tf_op jit(solution)/shard_map/ppermute | solution.py:49
  46.3 4.1 %collective-permute-start.1 = (bf16[256,512]{1,0:T(8,128)(2,1)S(1)}, bf16[256,512]{1,0:T(8,128)(2,1)S(1)}, u32[]{:S(2)}, u32[]{:S(2)}) collective-permute-start(bf16[256,512]{1,0:T(8,128)(2,1)S(1)} %get-tuple-element.27), channel_id=1, source_target_pairs={{0,0},{1,2},{2,4},{3,6},{4,1},{5,3},{6,5},{7,7},{8,8},{9,10},{10,1... | collective-permute-start | bytes 786440 | tf_op jit(solution)/shard_map/ppermute | solution.py:49
  50.4 0.1 pad_add_fusion.place._
  50.5 0.2 collective-permute-done.4.r3
  50.8 2.2 %collective-permute-done.3.r2 = bf16[256,512]{1,0:T(8,128)(2,1)S(1)} collective-permute-done((bf16[256,512]{1,0:T(8,128)(2,1)S(1)}, bf16[256,512]{1,0:T(8,128)(2,1)S(1)}, u32[]{:S(2)}, u32[]{:S(2)}) %collective-permute-start.3) | collective-permute-done | bytes 262176 | tf_op jit(solution)/shard_map/ppermute | solution.py:49
  53.0 5.0 %collective-permute-done.2.r1 = bf16[256,512]{1,0:T(8,128)(2,1)S(1)} collective-permute-done((bf16[256,512]{1,0:T(8,128)(2,1)S(1)}, bf16[256,512]{1,0:T(8,128)(2,1)S(1)}, u32[]{:S(2)}, u32[]{:S(2)}) %collective-permute-start.2) | collective-permute-done | bytes 262176 | tf_op jit(solution)/shard_map/ppermute | solution.py:49
  57.9 0.1 collective-permute-done.1.r0
  58.0 0.7 copy-done.9
  58.7 0.9 copy-done.10
  59.7 4.3 %weight_grad.1 = (bf16[8,128,512]{2,1,0:T(8,128)(2,1)}, bf16[8,48,512]{2,1,0:T(8,128)(2,1)S(1)}, bf16[8,48,512]{2,1,0:T(8,128)(2,1)}, bf16[8,48,512]{2,1,0:T(8,1...) custom-call(s32[3]{0:T(128)S(1)} %pad_add_fusion.place._, bf16[256,1280]{1,0:T(8,128)(2,1)S(1)} %copy-done.7, ...), custom_call_target="tpu_custom_call" | custom-call | flops 1342177280 | bytes 8388608 | tf_op jit(solution)/shard_map/weight_grad/pallas_call | solution.py:63
  64.0 1.0 copy-done.12
  65.0 0.1 all-to-all-done.first
  65.0 6.9 %all-to-all-start.2 = ((bf16[8,128,512]{2,1,0:T(8,128)(2,1)}), bf16[8,128,512]{2,1,0:T(8,128)(2,1)S(1)}, u32[]{:S(2)}, u32[]{:S(2)}) async-start(bf16[8,128,512]{2,1,0:T(8,128)(2,1)} %get-tuple-element.40), calls=%async_computation.2 | async-start | bytes 2097152 | tf_op jit(solution)/shard_map/all_to_all | solution.py:53
  71.9 4.1 %collective-permute-start.12 = (bf16[8,48,512]{2,1,0:T(8,128)(2,1)}, bf16[8,48,512]{2,1,0:T(8,128)(2,1)S(1)}, u32[]{:S(2)}, u32[]{:S(2)}) collective-permute-start(bf16[8,48,512]{2,1,0:T(8,128)(2,1)} %all-to-all-done.1), channel_id=1, source_target_pairs={{0,192},{1,64},{2,196},{3,68},{4,0},{5,128},{6,4},{7,132},{8,200},... | collective-permute-start | bytes 1179656 | tf_op jit(solution)/shard_map/ppermute | solution.py:49
  76.1 4.2 %collective-permute-start.11 = (bf16[8,48,512]{2,1,0:T(8,128)(2,1)}, bf16[8,48,512]{2,1,0:T(8,128)(2,1)S(1)}, u32[]{:S(2)}, u32[]{:S(2)}) collective-permute-start(bf16[8,48,512]{2,1,0:T(8,128)(2,1)} %all-to-all-done.1), channel_id=1, source_target_pairs={{0,128},{1,0},{2,132},{3,4},{4,192},{5,64},{6,196},{7,68},{8,136},... | collective-permute-start | bytes 1179656 | tf_op jit(solution)/shard_map/ppermute | solution.py:49
  80.3 1.9 collective-permute-start.10
  82.2 1.9 collective-permute-start.9
  84.2 7.3 %collective-permute-start.22 = (bf16[8,48,512]{2,1,0:T(8,128)(2,1)S(1)}, bf16[8,48,512]{2,1,0:T(8,128)(2,1)S(1)}, u32[]{:S(2)}, u32[]{:S(2)}) collective-permute-start(bf16[8,48,512]{2,1,0:T(8,128)(2,1)S(1)} %get-tuple-element.45), channel_id=1, source_target_pairs={{0,0},{1,64},{2,128},{3,192},{4,2},{5,66},{6,130},{7,194},{8,8},{9... | collective-permute-start | bytes 1179656 | tf_op jit(solution)/shard_map/ppermute | solution.py:49
  91.4 4.2 %collective-permute-start.23 = (bf16[8,48,512]{2,1,0:T(8,128)(2,1)}, bf16[8,48,512]{2,1,0:T(8,128)(2,1)S(1)}, u32[]{:S(2)}, u32[]{:S(2)}) collective-permute-start(bf16[8,48,512]{2,1,0:T(8,128)(2,1)} %get-tuple-element.46), channel_id=1, source_target_pairs={{0,4},{1,68},{2,132},{3,196},{4,6},{5,70},{6,134},{7,198},{8,12},{... | collective-permute-start | bytes 1179656 | tf_op jit(solution)/shard_map/ppermute | solution.py:49
  95.7 2.1 collective-permute-done.11.w2
  97.8 5.9 %collective-permute-done.10.w1 = bf16[8,48,512]{2,1,0:T(8,128)(2,1)S(1)} collective-permute-done((bf16[8,48,512]{2,1,0:T(8,128)(2,1)}, bf16[8,48,512]{2,1,0:T(8,128)(2,1)S(1)}, u32[]{:S(2)}, u32[]{:S(2)}) %collective-permute-start.10) | collective-permute-done | bytes 393248 | tf_op jit(solution)/shard_map/ppermute | solution.py:49
  103.7 4.7 %collective-permute-start.25 = (bf16[8,48,512]{2,1,0:T(8,128)(2,1)}, bf16[8,48,512]{2,1,0:T(8,128)(2,1)S(1)}, u32[]{:S(2)}, u32[]{:S(2)}) collective-permute-start(bf16[8,48,512]{2,1,0:T(8,128)(2,1)} %get-tuple-element.48), channel_id=1, source_target_pairs={{0,5},{1,69},{2,133},{3,197},{4,7},{5,71},{6,135},{7,199},{8,13},{... | collective-permute-start | bytes 1179656 | tf_op jit(solution)/shard_map/ppermute | solution.py:49
  108.5 0.8 collective-permute-done.9.w0
  109.2 3.7 %attn_grad.1 = (bf16[256,512]{1,0:T(8,128)(2,1)}, bf16[256,512]{1,0:T(8,128)(2,1)}, bf16[256,512]{1,0:T(8,128)(2,1)}, bf16[256,512]{1,0:T(8,128)(2,1)}, bf16[1280,1024]{1,0:T(8,128)(2,1)S(1)}) custom-call(s32[3]{0:T(128)S(1)} %pad_add_fusion.place._, bf16[256,1280]{1,0:T(8,128)(2,1)S(1)} %copy-done.8, bf16[256,1280]{1,0:T(8,128)(2,1)} %collective-permute-done.other, ...), custom_call_target="tpu_custom_call" | custom-call | flops 1342177280 | bytes 8388608 | tf_op jit(solution)/shard_map/attn_grad/pallas_call | solution.py:63
  112.9 2.9 %layer_out.1 = (f32[256,1280]{1,0:T(8,128)S(1)}, bf16[256,1280]{1,0:T(8,128)(2,1)}) custom-call(s32[3]{0:T(128)S(1)} %pad_add_fusion.place._, bf16[512,1024]{1,0:T(8,128)(2,1)S(1)} %copy-done.13, bf16[1280,1024]{1,0:T(8,128)(2,1)S(1)} %get-tuple-element.29.wt), custom_call_target="tpu_custom_call" | custom-call | flops 1342177280 | bytes 6291456 | tf_op jit(solution)/shard_map/layer_out/pallas_call | solution.py:63
  115.8 44.4 %collective-permute-done.22.b0 = bf16[8,48,512]{2,1,0:T(8,128)(2,1)S(1)} collective-permute-done((bf16[8,48,512]{2,1,0:T(8,128)(2,1)S(1)}, bf16[8,48,512]{2,1,0:T(8,128)(2,1)S(1)}, u32[]{:S(2)}, u32[]{:S(2)}) %collective-permute-start.22) | collective-permute-done | bytes 393248 | tf_op jit(solution)/shard_map/ppermute | solution.py:49
  160.3 1.9 collective-permute-start.14
  162.2 5.1 %collective-permute-start.15 = (bf16[256,512]{1,0:T(8,128)(2,1)}, bf16[256,512]{1,0:T(8,128)(2,1)S(1)}, u32[]{:S(2)}, u32[]{:S(2)}) collective-permute-start(bf16[256,512]{1,0:T(8,128)(2,1)} %get-tuple-element.33), channel_id=1, source_target_pairs={{0,4},{1,1},{2,5},{3,0},{4,6},{5,3},{6,7},{7,2},{8,12},{9,9},{10,1... | collective-permute-start | bytes 786440 | tf_op jit(solution)/shard_map/ppermute | solution.py:49
  167.4 6.7 %collective-permute-start.16 = (bf16[256,512]{1,0:T(8,128)(2,1)}, bf16[256,512]{1,0:T(8,128)(2,1)}, u32[]{:S(2)}, u32[]{:S(2)}) collective-permute-start(bf16[256,512]{1,0:T(8,128)(2,1)} %get-tuple-element.34), channel_id=1, source_target_pairs={{0,1},{1,5},{2,0},{3,4},{4,3},{5,7},{6,2},{7,6},{8,9},{9,13},{10,8... | collective-permute-start | bytes 786440 | tf_op jit(solution)/shard_map/ppermute | solution.py:49
  174.0 1.9 collective-permute-start.17
  175.9 1.5 sum_four.1
  177.4 6.6 %all-to-all-start.3 = ((bf16[8,48,512]{2,1,0:T(8,128)(2,1)}), bf16[8,48,512]{2,1,0:T(8,128)(2,1)S(1)}, u32[]{:S(2)}, u32[]{:S(2)}) async-start(bf16[8,48,512]{2,1,0:T(8,128)(2,1)} %sum_four.1), calls=%async_computation.3 | async-start | bytes 786432 | tf_op jit(solution)/shard_map/all_to_all | solution.py:53
  184.0 1.2 copy-done.1
  185.2 0.8 copy-done.4
  186.1 0.8 copy-done.6
  186.9 3.3 %attention_backward.1 = (bf16[256,512]{1,0:T(8,128)(2,1)}, bf16[256,128]{1,0:T(8,128)(2,1)}, bf16[256,128]{1,0:T(8,128)(2,1)}) custom-call(s32[3]{0:T(128)S(1)} %pad_add_fusion.place._, bf16[256,512]{1,0:T(8,128)(2,1)S(1)} %collective-permute-done.14.a0, bf16[256,512]{1,0:T(8,128)(2,1)S(1)} %collective-permute-done.15.a1, ...), custom_call_target="tpu_custom_call" | custom-call | flops 335544320 | bytes 3145728 | tf_op jit(solution)/shard_map/attention_backward/pallas_call | solution.py:63
  190.3 0.7 sum_z.1
  191.0 1.9 collective-permute-start.18
  192.9 1.9 collective-permute-start.19
  194.8 8.1 %collective-permute-start.20 = (bf16[32,512]{1,0:T(8,128)(2,1)S(1)}, bf16[32,512]{1,0:T(8,128)(2,1)S(1)}, u32[]{:S(2)}, u32[]{:S(2)}) collective-permute-start(bf16[32,512]{1,0:T(8,128)(2,1)S(1)} %get-tuple-element.43), channel_id=1, source_target_pairs={{0,1},{1,65},{2,129},{3,193},{4,3},{5,67},{6,131},{7,195},{8,9},{9... | collective-permute-start | bytes 98312 | tf_op jit(solution)/shard_map/ppermute | solution.py:49
  202.9 1.9 collective-permute-start.21
  204.9 2.0 add_convert_fusion
  206.9 4.8 %collective-permute-done.21.o3 = bf16[32,512]{1,0:T(8,128)(2,1)S(1)} collective-permute-done((bf16[32,512]{1,0:T(8,128)(2,1)S(1)}, bf16[32,512]{1,0:T(8,128)(2,1)S(1)}, u32[]{:S(2)}, u32[]{:S(2)}) %collective-permute-start.21) | collective-permute-done | bytes 32800 | tf_op jit(solution)/shard_map/ppermute | solution.py:49
  211.8 1.3 finish.1
  (39 shorter events, 0.1 us)
Async XLA Ops:
  2.2 25.5 %all-to-all-start.1 = ((bf16[8,48,512]{2,1,0:T(8,128)(2,1)}), bf16[8,48,512]{2,1,0:T(8,128)(2,1)}, u32[]{:S(2)}, u32[]{:S(2)}) async-start(bf16[8,48,512]{2,1,0:T(8,128)(2,1)} %broadcast_in_dim.5), calls=%async_computation.1 | async-start | bytes 786432 | tf_op jit(solution)/shard_map/all_to_all | solution.py:53
  11.2 11.2 %collective-permute-start.8 = (bf16[32,512]{1,0:T(8,128)(2,1)S(1)}, bf16[32,512]{1,0:T(8,128)(2,1)S(1)}, u32[]{:S(2)}, u32[]{:S(2)}) collective-permute-start(bf16[32,512]{1,0:T(8,128)(2,1)S(1)} %slice.11), channel_id=1, source_target_pairs={{0,192},{1,64},{2,196},{3,68},{4,0},{5,128},{6,4},{7,132},{8,200},... | collective-permute-start | bytes 98312 | tf_op jit(solution)/shard_map/ppermute | solution.py:49
  16.2 6.2 %collective-permute-start.7 = (bf16[32,512]{1,0:T(8,128)(2,1)S(1)}, bf16[32,512]{1,0:T(8,128)(2,1)S(1)}, u32[]{:S(2)}, u32[]{:S(2)}) collective-permute-start(bf16[32,512]{1,0:T(8,128)(2,1)S(1)} %slice.11), channel_id=1, source_target_pairs={{0,128},{1,0},{2,132},{3,4},{4,192},{5,64},{6,196},{7,68},{8,136},... | collective-permute-start | bytes 98312 | tf_op jit(solution)/shard_map/ppermute | solution.py:49
  17.2 9.2 %collective-permute-start.6 = (bf16[32,512]{1,0:T(8,128)(2,1)S(1)}, bf16[32,512]{1,0:T(8,128)(2,1)S(1)}, u32[]{:S(2)}, u32[]{:S(2)}) collective-permute-start(bf16[32,512]{1,0:T(8,128)(2,1)S(1)} %slice.11), channel_id=1, source_target_pairs={{0,64},{1,192},{2,68},{3,196},{4,128},{5,0},{6,132},{7,4},{8,72},{... | collective-permute-start | bytes 98312 | tf_op jit(solution)/shard_map/ppermute | solution.py:49
  19.2 8.6 %collective-permute-start.5 = (bf16[32,512]{1,0:T(8,128)(2,1)S(1)}, bf16[32,512]{1,0:T(8,128)(2,1)S(1)}, u32[]{:S(2)}, u32[]{:S(2)}) collective-permute-start(bf16[32,512]{1,0:T(8,128)(2,1)S(1)} %slice.11), channel_id=1, source_target_pairs={{0,0},{1,128},{2,4},{3,132},{4,64},{5,192},{6,68},{7,196},{8,8},{9... | collective-permute-start | bytes 98312 | tf_op jit(solution)/shard_map/ppermute | solution.py:49
  28.9 6.8 %copy-start.7 = (bf16[256,1280]{1,0:T(8,128)(2,1)S(1)}, bf16[256,1280]{1,0:T(8,128)(2,1)}, u32[]{:S(2)}) copy-start(bf16[256,1280]{1,0:T(8,128)(2,1)} %own.3) | copy-start | bytes 1966084
  28.9 6.9 %copy-start.2 = (bf16[256,512]{1,0:T(8,128)(2,1)S(1)}, bf16[256,512]{1,0:T(8,128)(2,1)}, u32[]{:S(2)}) copy-start(bf16[256,512]{1,0:T(8,128)(2,1)} %q_ref.3) | copy-start | bytes 786436
  28.9 6.9 %copy-start.3 = (bf16[256,128]{1,0:T(8,128)(2,1)S(1)}, bf16[256,128]{1,0:T(8,128)(2,1)}, u32[]{:S(2)}) copy-start(bf16[256,128]{1,0:T(8,128)(2,1)} %k_ref.3) | copy-start | bytes 196612
  28.9 6.9 %copy-start.5 = (bf16[256,128]{1,0:T(8,128)(2,1)S(1)}, bf16[256,128]{1,0:T(8,128)(2,1)}, u32[]{:S(2)}) copy-start(bf16[256,128]{1,0:T(8,128)(2,1)} %v_ref.3) | copy-start | bytes 196612
  28.9 6.9 %copy-start.11 = (s32[1,8]{1,0:T(1,128)S(1)}, s32[1,8]{1,0:T(1,128)}, u32[]{:S(2)}) copy-start(s32[1,8]{1,0:T(1,128)} %param.11) | copy-start | bytes 100
  28.9 36.2 %all-to-all-start = ((bf16[8,128,512]{2,1,0:T(8,128)(2,1)}), bf16[8,128,512]{2,1,0:T(8,128)(2,1)S(1)}, u32[]{:S(2)}, u32[]{:S(2)}) async-start(bf16[8,128,512]{2,1,0:T(8,128)(2,1)} %broadcast_in_dim.4), calls=%async_computation | async-start | bytes 2097152 | tf_op jit(solution)/shard_map/all_to_all | solution.py:53
  35.7 23.1 %collective-permute-start = (bf16[256,1280]{1,0:T(8,128)(2,1)S(1)}, bf16[256,1280]{1,0:T(8,128)(2,1)}, u32[]{:S(2)}, u32[]{:S(2)}) collective-permute-start(bf16[256,1280]{1,0:T(8,128)(2,1)S(1)} %copy-done.7), channel_id=1, source_target_pairs={{0,4},{1,5},{2,6},{3,7},{4,0},{5,1},{6,2},{7,3},{8,12},{9,13},{10,... | collective-permute-start | bytes 1966088 | tf_op jit(solution)/shard_map/ppermute | solution.py:49
  37.5 1.0 copy-start
  38.5 12.3 %collective-permute-start.4 = (bf16[256,512]{1,0:T(8,128)(2,1)S(1)}, bf16[256,512]{1,0:T(8,128)(2,1)S(1)}, u32[]{:S(2)}, u32[]{:S(2)}) collective-permute-start(bf16[256,512]{1,0:T(8,128)(2,1)S(1)} %get-tuple-element.27), channel_id=1, source_target_pairs={{0,3},{1,1},{2,7},{3,5},{4,0},{5,2},{6,4},{7,6},{8,11},{9,9},{10,1... | collective-permute-start | bytes 786440 | tf_op jit(solution)/shard_map/ppermute | solution.py:49
  41.5 11.5 %collective-permute-start.3 = (bf16[256,512]{1,0:T(8,128)(2,1)S(1)}, bf16[256,512]{1,0:T(8,128)(2,1)S(1)}, u32[]{:S(2)}, u32[]{:S(2)}) collective-permute-start(bf16[256,512]{1,0:T(8,128)(2,1)S(1)} %get-tuple-element.27), channel_id=1, source_target_pairs={{0,2},{1,0},{2,6},{3,4},{4,3},{5,1},{6,7},{7,5},{8,10},{9,8},{10,1... | collective-permute-start | bytes 786440 | tf_op jit(solution)/shard_map/ppermute | solution.py:49
  41.6 16.3 %collective-permute-start.2 = (bf16[256,512]{1,0:T(8,128)(2,1)S(1)}, bf16[256,512]{1,0:T(8,128)(2,1)S(1)}, u32[]{:S(2)}, u32[]{:S(2)}) collective-permute-start(bf16[256,512]{1,0:T(8,128)(2,1)S(1)} %get-tuple-element.27), channel_id=1, source_target_pairs={{0,1},{1,3},{2,5},{3,7},{4,2},{5,0},{6,6},{7,4},{8,9},{9,11},{10,1... | collective-permute-start | bytes 786440 | tf_op jit(solution)/shard_map/ppermute | solution.py:49
  46.3 11.7 %collective-permute-start.1 = (bf16[256,512]{1,0:T(8,128)(2,1)S(1)}, bf16[256,512]{1,0:T(8,128)(2,1)S(1)}, u32[]{:S(2)}, u32[]{:S(2)}) collective-permute-start(bf16[256,512]{1,0:T(8,128)(2,1)S(1)} %get-tuple-element.27), channel_id=1, source_target_pairs={{0,0},{1,2},{2,4},{3,6},{4,1},{5,3},{6,5},{7,7},{8,8},{9,10},{10,1... | collective-permute-start | bytes 786440 | tf_op jit(solution)/shard_map/ppermute | solution.py:49
  58.0 0.7 copy-start.9
  58.7 1.0 copy-start.10
  64.0 1.0 copy-start.12
  65.0 44.3 %copy-start.8 = (bf16[256,1280]{1,0:T(8,128)(2,1)S(1)}, bf16[256,1280]{1,0:T(8,128)(2,1)}, u32[]{:S(2)}) copy-start(bf16[256,1280]{1,0:T(8,128)(2,1)} %own.3) | copy-start | bytes 1966084
  65.0 112.4 %all-to-all-start.2 = ((bf16[8,128,512]{2,1,0:T(8,128)(2,1)}), bf16[8,128,512]{2,1,0:T(8,128)(2,1)S(1)}, u32[]{:S(2)}, u32[]{:S(2)}) async-start(bf16[8,128,512]{2,1,0:T(8,128)(2,1)} %get-tuple-element.40), calls=%async_computation.2 | async-start | bytes 2097152 | tf_op jit(solution)/shard_map/all_to_all | solution.py:53
  71.9 19.5 %collective-permute-start.12 = (bf16[8,48,512]{2,1,0:T(8,128)(2,1)}, bf16[8,48,512]{2,1,0:T(8,128)(2,1)S(1)}, u32[]{:S(2)}, u32[]{:S(2)}) collective-permute-start(bf16[8,48,512]{2,1,0:T(8,128)(2,1)} %all-to-all-done.1), channel_id=1, source_target_pairs={{0,192},{1,64},{2,196},{3,68},{4,0},{5,128},{6,4},{7,132},{8,200},... | collective-permute-start | bytes 1179656 | tf_op jit(solution)/shard_map/ppermute | solution.py:49
  76.1 21.7 %collective-permute-start.11 = (bf16[8,48,512]{2,1,0:T(8,128)(2,1)}, bf16[8,48,512]{2,1,0:T(8,128)(2,1)S(1)}, u32[]{:S(2)}, u32[]{:S(2)}) collective-permute-start(bf16[8,48,512]{2,1,0:T(8,128)(2,1)} %all-to-all-done.1), channel_id=1, source_target_pairs={{0,128},{1,0},{2,132},{3,4},{4,192},{5,64},{6,196},{7,68},{8,136},... | collective-permute-start | bytes 1179656 | tf_op jit(solution)/shard_map/ppermute | solution.py:49
  80.3 23.4 %collective-permute-start.10 = (bf16[8,48,512]{2,1,0:T(8,128)(2,1)}, bf16[8,48,512]{2,1,0:T(8,128)(2,1)S(1)}, u32[]{:S(2)}, u32[]{:S(2)}) collective-permute-start(bf16[8,48,512]{2,1,0:T(8,128)(2,1)} %all-to-all-done.1), channel_id=1, source_target_pairs={{0,64},{1,192},{2,68},{3,196},{4,128},{5,0},{6,132},{7,4},{8,72},{... | collective-permute-start | bytes 1179656 | tf_op jit(solution)/shard_map/ppermute | solution.py:49
  82.2 27.0 %collective-permute-start.9 = (bf16[8,48,512]{2,1,0:T(8,128)(2,1)}, bf16[8,48,512]{2,1,0:T(8,128)(2,1)S(1)}, u32[]{:S(2)}, u32[]{:S(2)}) collective-permute-start(bf16[8,48,512]{2,1,0:T(8,128)(2,1)} %all-to-all-done.1), channel_id=1, source_target_pairs={{0,0},{1,128},{2,4},{3,132},{4,64},{5,192},{6,68},{7,196},{8,8},{9... | collective-permute-start | bytes 1179656 | tf_op jit(solution)/shard_map/ppermute | solution.py:49
  84.2 76.1 %collective-permute-start.22 = (bf16[8,48,512]{2,1,0:T(8,128)(2,1)S(1)}, bf16[8,48,512]{2,1,0:T(8,128)(2,1)S(1)}, u32[]{:S(2)}, u32[]{:S(2)}) collective-permute-start(bf16[8,48,512]{2,1,0:T(8,128)(2,1)S(1)} %get-tuple-element.45), channel_id=1, source_target_pairs={{0,0},{1,64},{2,128},{3,192},{4,2},{5,66},{6,130},{7,194},{8,8},{9... | collective-permute-start | bytes 1179656 | tf_op jit(solution)/shard_map/ppermute | solution.py:49
  91.4 70.7 %collective-permute-start.23 = (bf16[8,48,512]{2,1,0:T(8,128)(2,1)}, bf16[8,48,512]{2,1,0:T(8,128)(2,1)S(1)}, u32[]{:S(2)}, u32[]{:S(2)}) collective-permute-start(bf16[8,48,512]{2,1,0:T(8,128)(2,1)} %get-tuple-element.46), channel_id=1, source_target_pairs={{0,4},{1,68},{2,132},{3,196},{4,6},{5,70},{6,134},{7,198},{8,12},{... | collective-permute-start | bytes 1179656 | tf_op jit(solution)/shard_map/ppermute | solution.py:49
  97.8 69.6 %collective-permute-start.24 = (bf16[8,48,512]{2,1,0:T(8,128)(2,1)}, bf16[8,48,512]{2,1,0:T(8,128)(2,1)S(1)}, u32[]{:S(2)}, u32[]{:S(2)}) collective-permute-start(bf16[8,48,512]{2,1,0:T(8,128)(2,1)} %get-tuple-element.47), channel_id=1, source_target_pairs={{0,1},{1,65},{2,129},{3,193},{4,3},{5,67},{6,131},{7,195},{8,9},{9... | collective-permute-start | bytes 1179656 | tf_op jit(solution)/shard_map/ppermute | solution.py:49
  103.7 9.2 %copy-start.13 = (bf16[512,1024]{1,0:T(8,128)(2,1)S(1)}, bf16[512,1024]{1,0:T(8,128)(2,1)}, u32[]{:S(2)}) copy-start(bf16[512,1024]{1,0:T(8,128)(2,1)} %copy-done.12) | copy-start | bytes 3145732
  103.7 70.3 %collective-permute-start.25 = (bf16[8,48,512]{2,1,0:T(8,128)(2,1)}, bf16[8,48,512]{2,1,0:T(8,128)(2,1)S(1)}, u32[]{:S(2)}, u32[]{:S(2)}) collective-permute-start(bf16[8,48,512]{2,1,0:T(8,128)(2,1)} %get-tuple-element.48), channel_id=1, source_target_pairs={{0,5},{1,69},{2,133},{3,197},{4,7},{5,71},{6,135},{7,199},{8,13},{... | collective-permute-start | bytes 1179656 | tf_op jit(solution)/shard_map/ppermute | solution.py:49
  115.8 89.0 %collective-permute-start.13 = (bf16[256,1280]{1,0:T(8,128)(2,1)}, bf16[256,1280]{1,0:T(8,128)(2,1)}, u32[]{:S(2)}, u32[]{:S(2)}) collective-permute-start(bf16[256,1280]{1,0:T(8,128)(2,1)} %get-tuple-element.31), channel_id=1, source_target_pairs={{0,4},{1,5},{2,6},{3,7},{4,0},{5,1},{6,2},{7,3},{8,12},{9,13},{10,... | collective-permute-start | bytes 1966088 | tf_op jit(solution)/shard_map/ppermute | solution.py:49
  160.3 23.7 %collective-permute-start.14 = (bf16[256,512]{1,0:T(8,128)(2,1)}, bf16[256,512]{1,0:T(8,128)(2,1)S(1)}, u32[]{:S(2)}, u32[]{:S(2)}) collective-permute-start(bf16[256,512]{1,0:T(8,128)(2,1)} %get-tuple-element.32), channel_id=1, source_target_pairs={{0,0},{1,4},{2,1},{3,5},{4,2},{5,6},{6,3},{7,7},{8,8},{9,12},{10,9... | collective-permute-start | bytes 786440 | tf_op jit(solution)/shard_map/ppermute | solution.py:49
  162.2 21.8 %collective-permute-start.15 = (bf16[256,512]{1,0:T(8,128)(2,1)}, bf16[256,512]{1,0:T(8,128)(2,1)S(1)}, u32[]{:S(2)}, u32[]{:S(2)}) collective-permute-start(bf16[256,512]{1,0:T(8,128)(2,1)} %get-tuple-element.33), channel_id=1, source_target_pairs={{0,4},{1,1},{2,5},{3,0},{4,6},{5,3},{6,7},{7,2},{8,12},{9,9},{10,1... | collective-permute-start | bytes 786440 | tf_op jit(solution)/shard_map/ppermute | solution.py:49
  167.4 16.6 %collective-permute-start.16 = (bf16[256,512]{1,0:T(8,128)(2,1)}, bf16[256,512]{1,0:T(8,128)(2,1)}, u32[]{:S(2)}, u32[]{:S(2)}) collective-permute-start(bf16[256,512]{1,0:T(8,128)(2,1)} %get-tuple-element.34), channel_id=1, source_target_pairs={{0,1},{1,5},{2,0},{3,4},{4,3},{5,7},{6,2},{7,6},{8,9},{9,13},{10,8... | collective-permute-start | bytes 786440 | tf_op jit(solution)/shard_map/ppermute | solution.py:49
  174.0 10.0 %collective-permute-start.17 = (bf16[256,512]{1,0:T(8,128)(2,1)}, bf16[256,512]{1,0:T(8,128)(2,1)}, u32[]{:S(2)}, u32[]{:S(2)}) collective-permute-start(bf16[256,512]{1,0:T(8,128)(2,1)} %get-tuple-element.35), channel_id=1, source_target_pairs={{0,5},{1,0},{2,4},{3,1},{4,7},{5,2},{6,6},{7,3},{8,13},{9,8},{10,1... | collective-permute-start | bytes 786440 | tf_op jit(solution)/shard_map/ppermute | solution.py:49
  177.4 29.5 %all-to-all-start.3 = ((bf16[8,48,512]{2,1,0:T(8,128)(2,1)}), bf16[8,48,512]{2,1,0:T(8,128)(2,1)S(1)}, u32[]{:S(2)}, u32[]{:S(2)}) async-start(bf16[8,48,512]{2,1,0:T(8,128)(2,1)} %sum_four.1), calls=%async_computation.3 | async-start | bytes 786432 | tf_op jit(solution)/shard_map/all_to_all | solution.py:53
  184.0 1.2 copy-start.1
  185.2 0.8 copy-start.4
  186.1 0.8 copy-start.6
  191.0 16.0 %collective-permute-start.18 = (bf16[32,512]{1,0:T(8,128)(2,1)S(1)}, bf16[32,512]{1,0:T(8,128)(2,1)S(1)}, u32[]{:S(2)}, u32[]{:S(2)}) collective-permute-start(bf16[32,512]{1,0:T(8,128)(2,1)S(1)} %get-tuple-element.41), channel_id=1, source_target_pairs={{0,0},{1,64},{2,128},{3,192},{4,2},{5,66},{6,130},{7,194},{8,8},{9... | collective-permute-start | bytes 98312 | tf_op jit(solution)/shard_map/ppermute | solution.py:49
  192.9 14.0 %collective-permute-start.19 = (bf16[32,512]{1,0:T(8,128)(2,1)S(1)}, bf16[32,512]{1,0:T(8,128)(2,1)S(1)}, u32[]{:S(2)}, u32[]{:S(2)}) collective-permute-start(bf16[32,512]{1,0:T(8,128)(2,1)S(1)} %get-tuple-element.42), channel_id=1, source_target_pairs={{0,4},{1,68},{2,132},{3,196},{4,6},{5,70},{6,134},{7,198},{8,12},{... | collective-permute-start | bytes 98312 | tf_op jit(solution)/shard_map/ppermute | solution.py:49
  194.8 12.1 %collective-permute-start.20 = (bf16[32,512]{1,0:T(8,128)(2,1)S(1)}, bf16[32,512]{1,0:T(8,128)(2,1)S(1)}, u32[]{:S(2)}, u32[]{:S(2)}) collective-permute-start(bf16[32,512]{1,0:T(8,128)(2,1)S(1)} %get-tuple-element.43), channel_id=1, source_target_pairs={{0,1},{1,65},{2,129},{3,193},{4,3},{5,67},{6,131},{7,195},{8,9},{9... | collective-permute-start | bytes 98312 | tf_op jit(solution)/shard_map/ppermute | solution.py:49
  202.9 8.8 %collective-permute-start.21 = (bf16[32,512]{1,0:T(8,128)(2,1)S(1)}, bf16[32,512]{1,0:T(8,128)(2,1)S(1)}, u32[]{:S(2)}, u32[]{:S(2)}) collective-permute-start(bf16[32,512]{1,0:T(8,128)(2,1)S(1)} %get-tuple-element.44), channel_id=1, source_target_pairs={{0,5},{1,69},{2,133},{3,197},{4,7},{5,71},{6,135},{7,199},{8,13},{... | collective-permute-start | bytes 98312 | tf_op jit(solution)/shard_map/ppermute | solution.py:49

commit v2 on v1

v2 whole, which is shorter than its diff:
```python
import jax
import jax.numpy as jnp
from jax import lax
from jax.experimental import pallas as pl
from jax.experimental.pallas import tpu as pltpu
from jax.sharding import PartitionSpec as P


NX, NZ, NC, NY = 4, 8, 2, 4
HEAD = 128
TOK = 256
HEADS = 4
GROUP = HEADS * HEAD
COLS = 1280
SHARD = 80
FIRST = 48
REST = SHARD - FIRST
AXES = ("dp", "mp")
BF, F32 = jnp.bfloat16, jnp.float32
SCALE = HEAD ** -0.5


def route(target):
    pairs = []
    for x in range(NX):
        for z in range(NZ):
            for c in range(NC):
                for y in range(NY):
                    tx, tz, tc, ty = target(x, z, c, y)
                    src = ((x * NZ + z) * NC + c) * NY + y
                    pairs.append((src, ((tx * NZ + tz) * NC + tc) * NY + ty))
    return pairs


SWAP = route(lambda x, z, c, y: (x, z, 1 - c, y))
TO_PLANE = route(lambda x, z, c, y: (2 * (y % 2) + c, z, y // 2, x))
TO_OWNER = route(lambda x, z, c, y: (y, z, x % 2, 2 * c + x // 2))
HEADS_OUT = [route(lambda x, z, c, y, k=k: (x, z, y // 2, (2 * (y % 2) + c + k) % 4)) for k in range(4)]
HEADS_BACK = [
    route(lambda x, z, c, y, k=k: (x, z, (y + k) % 4 % 2, 2 * c + (y + k) % 4 // 2)) for k in range(4)
]
Z_GROUPS = [[(x * NZ + z) * NC + c for z in range(NZ)] for x in range(NX) for c in range(NC)]
X_GROUPS = [[(x * NZ + z) * NC + c for x in range(NX)] for z in range(NZ) for c in range(NC)]


def send(value, pairs):
    return lax.ppermute(value, AXES, pairs)


def exchange(blocks, groups):
    return lax.all_to_all(blocks, "dp", 0, 0, axis_index_groups=groups, tiled=True)


def gather(block, groups):
    return lax.all_gather(block, "dp", axis_index_groups=groups, tiled=True)


def scatter(blocks, groups):
    return lax.psum_scatter(blocks, "dp", axis_index_groups=groups, tiled=True)


def to_all(block, groups):
    return exchange(jnp.broadcast_to(block[None], (len(groups[0]), *block.shape)), groups)


def dot(a, b, dims):
    return lax.dot_general(a, b, (dims, ((), ())), preferred_element_type=F32)


def call(body, outs, scratch=(), flops=0, moved=0):
    def run(scalars, *operands):
        vmem = pl.BlockSpec(memory_space=pltpu.VMEM)
        return pl.pallas_call(
            body,
            out_shape=outs,
            in_specs=[pl.BlockSpec(memory_space=pltpu.SMEM)] + [vmem] * len(operands),
            out_specs=jax.tree.map(lambda _: vmem, outs),
            scratch_shapes=list(scratch),
            compiler_params=pltpu.CompilerParams(vmem_limit_bytes=40 << 20),
            cost_estimate=pl.CostEstimate(flops=flops, bytes_accessed=moved, transcendentals=0),
        )(scalars, *operands)

    return run


def shape(*dims, dtype=BF):
    return jax.ShapeDtypeStruct(dims, dtype)


def forward_body(lengths, q_ref, k_ref, v_ref, att_ref, prob_ref):
    rows = lax.broadcasted_iota(jnp.int32, (TOK, TOK), 0)
    cols = lax.broadcasted_iota(jnp.int32, (TOK, TOK), 1)
    row_at = lax.broadcasted_iota(jnp.int32, (TOK, 1), 0)
    col_at = lax.broadcasted_iota(jnp.int32, (1, TOK), 1)
    row_seg = jnp.zeros((TOK, 1), jnp.int32)
    col_seg = jnp.zeros((1, TOK), jnp.int32)
    end = jnp.int32(0)
    for i in range(8):
        end = end + lengths[i]
        row_seg = row_seg + (row_at >= end).astype(jnp.int32)
        col_seg = col_seg + (col_at >= end).astype(jnp.int32)
    allowed = (row_seg == col_seg) & (rows >= cols)
    for h in range(HEADS):
        at = slice(h * HEAD, (h + 1) * HEAD)
        logits = dot(q_ref[:, at], k_ref[...], ((1,), (1,))) * SCALE
        logits = jnp.where(allowed, logits, -jnp.inf)
        terms = jnp.exp(logits - jnp.max(logits, axis=-1, keepdims=True))
        prob = terms / jnp.sum(terms, axis=-1, keepdims=True)
        prob_ref[h] = prob
        att_ref[:, at] = dot(prob.astype(BF), v_ref[...], ((1,), (0,))).astype(BF)


def backward_body(_, a0, a1, a2, a3, q_ref, k_ref, v_ref, prob_ref, dq_ref, dk_ref, dv_ref):
    key_sum = jnp.zeros((TOK, HEAD), F32)
    value_sum = jnp.zeros((TOK, HEAD), F32)
    for h in range(HEADS):
        at = slice(h * HEAD, (h + 1) * HEAD)
        up = (
            (a0[:, at].astype(F32) + a1[:, at].astype(F32))
            + (a2[:, at].astype(F32) + a3[:, at].astype(F32))
        ).astype(BF)
        prob = prob_ref[h]
        prob_grad = dot(up, v_ref[...], ((1,), (1,)))
        delta = jnp.sum(prob * prob_grad, axis=-1, keepdims=True)
        score = (prob * (prob_grad - delta) * SCALE).astype(BF)
        dq_ref[:, at] = dot(score, k_ref[...], ((1,), (0,))).astype(BF)
        key_sum = key_sum + dot(score, q_ref[:, at], ((0,), (0,)))
        value_sum = value_sum + dot(prob.astype(BF), up, ((0,), (0,)))
    dk_ref[...] = key_sum.astype(BF)
    dv_ref[...] = value_sum.astype(BF)


def weight_grad_body(place, own, other, r0, r1, r2, r3, first_ref, rest_ref, att_ref, og, total):
    c, y = place[0], place[1]
    og[pl.ds(pl.multiple_of(c * TOK, TOK), TOK), :] = own[...]
    og[pl.ds(pl.multiple_of((1 - c) * TOK, TOK), TOK), :] = other[...]
    for k, ref in enumerate((r0, r1, r2, r3)):
        j = (y + 4 - k) % 4
        att_ref[
            pl.ds(pl.multiple_of((j % 2) * TOK, TOK), TOK),
            pl.ds(pl.multiple_of((j // 2) * GROUP, GROUP), GROUP),
        ] = ref[...]
    for i in range(COLS // 256):
        total[i * 256 : (i + 1) * 256, :] = dot(
            og[:, i * 256 : (i + 1) * 256], att_ref[...], ((0,), (0,))
        ).astype(BF)
    for z in range(NZ):
        for j in range(4):
            base = z * 160 + (j % 2) * SHARD
            lanes = slice((j // 2) * GROUP, (j // 2 + 1) * GROUP)
            first_ref[z, j] = total[base : base + FIRST, lanes]
            rest_ref[j, z] = total[base + FIRST : base + SHARD, lanes]


def attn_grad_body(place, own, other, first, rest, g0, g1, g2, g3, wt_ref, og):
    c, y = place[0], place[1]
    og[pl.ds(pl.multiple_of(c * TOK, TOK), TOK), :] = own[...]
    og[pl.ds(pl.multiple_of((1 - c) * TOK, TOK), TOK), :] = other[...]
    for z in range(NZ):
        for j in range(4):
            base = z * 160 + (j % 2) * SHARD
            lanes = slice((j // 2) * GROUP, (j // 2 + 1) * GROUP)
            wt_ref[base : base + FIRST, lanes] = first[z, j]
            wt_ref[base + FIRST : base + SHARD, lanes] = rest[j, z]
    for k, ref in enumerate((g0, g1, g2, g3)):
        m = (y + k) % 4
        ref[...] = dot(
            og[pl.ds(pl.multiple_of((m % 2) * TOK, TOK), TOK), :],
            wt_ref[:, pl.ds(pl.multiple_of((m // 2) * GROUP, GROUP), GROUP)],
            ((1,), (0,)),
        ).astype(BF)


def layer_out_body(place, att, wt, mine_ref, theirs_ref):
    c = place[0]
    mine_ref[...] = dot(att[pl.ds(pl.multiple_of(c * TOK, TOK), TOK), :], wt[...], ((1,), (1,)))
    theirs_ref[...] = dot(
        att[pl.ds(pl.multiple_of((1 - c) * TOK, TOK), TOK), :], wt[...], ((1,), (1,))
    ).astype(BF)


def sum_x_body(_, blocks, out):
    for z in range(NZ):
        out[z] = (
            (blocks[0, z].astype(F32) + blocks[1, z].astype(F32))
            + (blocks[2, z].astype(F32) + blocks[3, z].astype(F32))
        ).astype(BF)


def sum_z_body(_, first, blocks, out):
    out[:FIRST, :] = first[...]
    total = blocks[0].astype(F32)
    for z in range(1, NZ):
        total = total + blocks[z].astype(F32)
    out[FIRST:, :] = total.astype(BF)


def per_device(query_rows, key_rows, value_matrix, out_weight, out_grad, doc_lengths):
    dp, y = lax.axis_index("dp"), lax.axis_index("mp")
    place = jnp.stack([dp % NC, y]).astype(jnp.int32)
    wt = send(out_weight.T, TO_PLANE)
    rest_w = to_all(to_all(wt[FIRST:], Z_GROUPS), X_GROUPS)
    first_w = gather(to_all(wt[:FIRST], X_GROUPS).reshape(-1, GROUP), Z_GROUPS)
    other_grad = send(out_grad, SWAP)

    attended, prob = call(
        forward_body,
        (shape(TOK, GROUP), shape(HEADS, TOK, TOK, dtype=F32)),
        flops=4 * 4 * TOK * TOK * HEAD,
        moved=2 << 20,
    )(doc_lengths[0], query_rows, key_rows, value_matrix)
    heads = [send(attended, pairs) for pairs in HEADS_OUT]

    big = 2 * 2 * TOK * COLS * 2 * GROUP
    first_part, rest_part, attended_two = call(
        weight_grad_body,
        (shape(NZ, 4, FIRST, GROUP), shape(4, NZ, REST, GROUP), shape(2 * TOK, 2 * GROUP)),
        scratch=(pltpu.VMEM((2 * TOK, COLS), BF), pltpu.VMEM((COLS, 2 * GROUP), BF)),
        flops=big,
        moved=8 << 20,
    )(place, out_grad, other_grad, *heads)

    *partials, wt_two = call(
        attn_grad_body,
        (shape(TOK, GROUP),) * 4 + (shape(COLS, 2 * GROUP),),
        scratch=(pltpu.VMEM((2 * TOK, COLS), BF),),
        flops=big,
        moved=8 << 20,
    )(
        place,
        out_grad,
        other_grad,
        first_w.reshape(NZ, 4, FIRST, GROUP),
        rest_w.reshape(4, NZ, REST, GROUP),
    )
    upstream = [send(partial, pairs) for partial, pairs in zip(partials, HEADS_BACK)]

    mine, theirs = call(
        layer_out_body, (shape(TOK, COLS, dtype=F32), shape(TOK, COLS)), flops=big, moved=6 << 20
    )(place, attended_two, wt_two)
    layer_out = (mine + send(theirs, SWAP).astype(F32)).astype(BF)

    first_sum = scatter(scatter(first_part.reshape(-1, GROUP), Z_GROUPS), X_GROUPS)
    rest_sum = call(sum_x_body, shape(NZ, REST, GROUP), moved=2 << 20)(
        place, exchange(rest_part, X_GROUPS)
    )
    rest_sum = exchange(rest_sum, Z_GROUPS)
    weight_grad = call(sum_z_body, shape(SHARD, GROUP), moved=1 << 20)(place, first_sum, rest_sum)
    weight_grad = send(weight_grad, TO_OWNER).astype(F32)

    query_grad, key_grad, value_grad = call(
        backward_body,
        (shape(TOK, GROUP), shape(TOK, HEAD), shape(TOK, HEAD)),
        flops=5 * 4 * 2 * TOK * TOK * HEAD,
        moved=3 << 20,
    )(place, *upstream, query_rows, key_rows, value_matrix, prob)
    return (layer_out, query_grad, key_grad, value_grad, weight_grad.T)


def solution(mesh):
    placed = (
        P("dp", "mp"),
        P("dp", "mp"),
        P("dp", "mp"),
        P("mp", "dp"),
        P("dp", "mp"),
        P("dp", None),
    )
    return jax.shard_map(
        per_device,
        mesh=mesh,
        in_specs=placed,
        out_specs=(P("dp", "mp"), P("dp", "mp"), P("dp", "mp"), P("dp", "mp"), P("mp", "dp")),
        check_vma=False,
    )
```

time: 214 us -> 161 us (0.75)
  the two profiles are of different devices: /device:TPU:15 before, /device:TPU:8 now
where the time goes in v2:
time: 161 us; the launch traced here: 160 us
  blocking collectives  44.8 us (28%)
  starting transfers between devices  38 us (24%)
  waiting for transfers between devices  33.4 us (21%)
  Pallas kernels  16.1 us (10%)
  between operations  14 us (9%)
  local copies, waits for them, and re-layouts  10.5 us (7%)
  other arithmetic  2.83 us (2%)
    all_to_all x3, blocking collectives, exchange(): lax.all_to_all(blocks, 'dp', 0, 0, axis_index_groups=groups, tiled=True)  44.8 us
    ppermute x12, starting transfers between devices, send(): return lax.ppermute(value, AXES, pairs)  28.8 us
    ppermute x12, waiting for transfers between devices, send(): return lax.ppermute(value, AXES, pairs)  24.6 us
    pallas_call x7, Pallas kernels, run(): pl.pallas_call(body, out_shape=outs, in_specs=[pl.BlockSpec(memory_space=...  16.1 us
    unnamed x38, local copies, waits for them, and re-layouts  10.4 us
    all_to_all x2, starting transfers between devices, exchange(): lax.all_to_all(blocks, 'dp', 0, 0, axis_index_groups=groups, tiled=True)  9.08 us
    reduce_scatter x2, waiting for transfers between devices, scatter(): return lax.psum_scatter(blocks, 'dp', axis_index_groups=groups, tiled=True)  6.56 us
  transfers between devices with their start and end apart: 17, of which 9 were waited for; matrix products, arithmetic and copies ran while one was open for 1% of the time, Pallas kernels for 10%

profile of v2, /device:TPU:8, one launch (start us, length us, event | category | flops | bytes accessed | tf_op | source)
XLA Modules:
  0.0 159.6 jit_solution(478498568473895994)
XLA Ops:
  7.2 0.0 copy-start.8
  7.2 0.0 all-gather.2.cloned.1.call-start
  7.2 4.9 %collective-permute-start.5 = (bf16[80,512]{1,0:T(8,128)(2,1)}, bf16[80,512]{1,0:T(8,128)(2,1)S(1)}, u32[]{:S(2)}, u32[]{:S(2)}) collective-permute-start(bf16[80,512]{1,0:T(8,128)(2,1)} %bitcast.12), channel_id=1, source_target_pairs={{0,0},{1,128},{2,4},{3,132},{4,64},{5,192},{6,68},{7,196},{8,8},{9... | collective-permute-start | bytes 245768 | tf_op jit(solution)/shard_map/ppermute | solution.py:47
  12.2 2.6 %collective-permute-done.5 = bf16[80,512]{1,0:T(8,128)(2,1)S(1)} collective-permute-done((bf16[80,512]{1,0:T(8,128)(2,1)}, bf16[80,512]{1,0:T(8,128)(2,1)S(1)}, u32[]{:S(2)}, u32[]{:S(2)}) %collective-permute-start.5) | collective-permute-done | bytes 81952 | tf_op jit(solution)/shard_map/ppermute | solution.py:47
  14.8 10.9 %all_to_all.25 = bf16[4,48,512]{2,1,0:T(8,128)(2,1)} all-to-all(bf16[4,48,512]{2,1,0:T(8,128)(2,1)S(1)} %broadcast_in_dim.6), channel_id=1, replica_groups={{0,64,128,192},{4,68,132,196},{8,72,136,200},{12,76,140,204},{16,80,144..., dimensions={0} | all-to-all | bytes 393216 | tf_op jit(solution)/shard_map/all_to_all | solution.py:51
  25.7 0.0 all-gather.2.cloned.1.call-update
  25.8 0.0 reduce-scatter.3.cloned.1.call-start
  25.8 0.4 collective-permute-start
  26.3 0.9 copy-done
  27.2 0.8 copy-done.2
  28.0 0.8 copy-done.4
  28.9 0.7 copy-done.16
  29.5 1.7 %shard_map.101 = (bf16[256,512]{1,0:T(8,128)(2,1)S(1)}, f32[4,256,256]{2,1,0:T(8,128)S(1)}) custom-call(s32[8]{0:T(128)S(1)} %bitcast.10, bf16[256,512]{1,0:T(8,128)(2,1)S(1)} %copy-done, bf16[256,128]{1,0:T(8,128)(2,1)S(1)} %copy-done.2, bf16[256,128]{1,0:T(8,128)(2,1)S(1)} %copy-done.4), custom_call_target="tpu_custom_call" | custom-call | flops 134217728 | bytes 2097152 | tf_op jit(solution)/shard_map/pallas_call | solution.py:73
  31.2 0.7 collective-permute-start.4
  31.9 6.2 %collective-permute-start.3 = (bf16[256,512]{1,0:T(8,128)(2,1)S(1)}, bf16[256,512]{1,0:T(8,128)(2,1)S(1)}, u32[]{:S(2)}, u32[]{:S(2)}) collective-permute-start(bf16[256,512]{1,0:T(8,128)(2,1)S(1)} %get-tuple-element.20), channel_id=1, source_target_pairs={{0,2},{1,0},{2,6},{3,4},{4,3},{5,1},{6,7},{7,5},{8,10},{9,8},{10,1... | collective-permute-start | bytes 786440 | tf_op jit(solution)/shard_map/ppermute | solution.py:47
  38.1 1.9 %collective-permute-start.2 = (bf16[256,512]{1,0:T(8,128)(2,1)S(1)}, bf16[256,512]{1,0:T(8,128)(2,1)S(1)}, u32[]{:S(2)}, u32[]{:S(2)}) collective-permute-start(bf16[256,512]{1,0:T(8,128)(2,1)S(1)} %get-tuple-element.20), channel_id=1, source_target_pairs={{0,1},{1,3},{2,5},{3,7},{4,2},{5,0},{6,6},{7,4},{8,9},{9,11},{10,1... | collective-permute-start | bytes 786440 | tf_op jit(solution)/shard_map/ppermute | solution.py:47
  40.0 1.9 %collective-permute-start.1 = (bf16[256,512]{1,0:T(8,128)(2,1)S(1)}, bf16[256,512]{1,0:T(8,128)(2,1)}, u32[]{:S(2)}, u32[]{:S(2)}) collective-permute-start(bf16[256,512]{1,0:T(8,128)(2,1)S(1)} %get-tuple-element.20), channel_id=1, source_target_pairs={{0,0},{1,2},{2,4},{3,6},{4,1},{5,3},{6,5},{7,7},{8,8},{9,10},{10,1... | collective-permute-start | bytes 786440 | tf_op jit(solution)/shard_map/ppermute | solution.py:47
  42.0 0.1 pad_add_fusion.place._
  42.0 0.0 collective-permute-done.4.r3
  42.0 0.0 collective-permute-done.3.r2
  42.0 9.1 %collective-permute-done.2.r1 = bf16[256,512]{1,0:T(8,128)(2,1)S(1)} collective-permute-done((bf16[256,512]{1,0:T(8,128)(2,1)S(1)}, bf16[256,512]{1,0:T(8,128)(2,1)S(1)}, u32[]{:S(2)}, u32[]{:S(2)}) %collective-permute-start.2) | collective-permute-done | bytes 262176 | tf_op jit(solution)/shard_map/ppermute | solution.py:47
  51.1 1.4 collective-permute-done.1.r0
  52.5 4.4 %shard_map.102 = (bf16[8,4,48,512]{3,2,1,0:T(8,128)(2,1)}, bf16[4,8,32,512]{3,2,1,0:T(8,128)(2,1)}, bf16[512,1024]{1,0:T(8,128)(2,1)S(1)}) custom-call(s32[2]{0:T(128)S(1)} %pad_add_fusion.place._, bf16[256,1280]{1,0:T(8,128)(2,1)S(1)} %copy-done.8, bf16[256,1280]{1,0:T(8,128)(2,1)S(1)} %collective-permute-done.other, ...), custom_call_target="tpu_custom_call" | custom-call | flops 1342177280 | bytes 8388608 | tf_op jit(solution)/shard_map/pallas_call | solution.py:73
  57.0 1.0 copy-done.17
  58.0 0.0 reduce-scatter.3.cloned.1.call-update
  58.0 19.0 %all_to_all.26 = bf16[8,32,512]{2,1,0:T(8,128)(2,1)S(1)} all-to-all(bf16[8,32,512]{2,1,0:T(8,128)(2,1)S(1)} %broadcast_in_dim.7), channel_id=1, replica_groups={{0,8,16,24,32,40,48,56},{4,12,20,28,36,44,52,60},{64,72,80,88,96,104,11..., dimensions={0} | all-to-all | bytes 524288 | tf_op jit(solution)/shard_map/all_to_all | solution.py:51
  77.1 0.1 broadcast_in_dim.8
  77.2 14.8 %all_to_all.27.rest = bf16[4,8,32,512]{3,2,1,0:T(8,128)(2,1)S(1)} all-to-all(bf16[4,8,32,512]{3,2,1,0:T(8,128)(2,1)S(1)} %broadcast_in_dim.8), channel_id=1, replica_groups={{0,64,128,192},{4,68,132,196},{8,72,136,200},{12,76,140,204},{16,80,144..., dimensions={0} | all-to-all | bytes 2097152 | tf_op jit(solution)/shard_map/all_to_all | solution.py:51
  92.0 3.5 %all-to-all-start.3 = ((bf16[4,8,32,512]{3,2,1,0:T(8,128)(2,1)}), bf16[4,8,32,512]{3,2,1,0:T(8,128)(2,1)S(1)}, u32[]{:S(2)}, u32[]{:S(2)}) async-start(bf16[4,8,32,512]{3,2,1,0:T(8,128)(2,1)} %get-tuple-element.34), calls=%async_computation.5 | async-start | bytes 2097152 | tf_op jit(solution)/shard_map/all_to_all | solution.py:51
  95.5 0.0 all-gather.2.cloned.1.call-done
  95.6 1.4 copy-done.7
  97.0 1.1 copy-done.9
  98.1 1.1 copy-done.11
  99.2 2.3 %shard_map.103 = (bf16[256,512]{1,0:T(8,128)(2,1)S(1)}, bf16[256,512]{1,0:T(8,128)(2,1)S(1)}, bf16[256,512]{1,0:T(8,128)(2,1)S(1)}, bf16[256,512]{1,0:T(8,128)(2,1)S(1)}, bf16[1280,1024]{1,0:T(8,128)(2,1)S(1)}) custom-call(s32[2]{0:T(128)S(1)} %pad_add_fusion.place._, bf16[256,1280]{1,0:T(8,128)(2,1)S(1)} %copy-done.9, bf16[256,1280]{1,0:T(8,128)(2,1)S(1)} %copy-done.11, ...), custom_call_target="tpu_custom_call" | custom-call | flops 1342177280 | bytes 8388608 | tf_op jit(solution)/shard_map/pallas_call | solution.py:73
  101.5 0.0 copy-start.15
  101.5 0.7 copy-done.15
  102.2 2.9 %shard_map.104 = (f32[256,1280]{1,0:T(8,128)S(1)}, bf16[256,1280]{1,0:T(8,128)(2,1)}) custom-call(s32[2]{0:T(128)S(1)} %pad_add_fusion.place._, bf16[512,1024]{1,0:T(8,128)(2,1)S(1)} %copy-done.18, bf16[1280,1024]{1,0:T(8,128)(2,1)S(1)} %get-tuple-element.22.wt), custom_call_target="tpu_custom_call" | custom-call | flops 1342177280 | bytes 6291456 | tf_op jit(solution)/shard_map/pallas_call | solution.py:73
  105.2 0.0 copy-start.3
  105.2 0.0 copy-start.5
  105.2 0.1 collective-permute-start.6
  105.3 1.5 all-to-all-done.3.blocks
  106.8 1.4 shard_map.106
  108.2 5.6 %all-to-all-start.4 = ((bf16[8,32,512]{2,1,0:T(8,128)(2,1)}), bf16[8,32,512]{2,1,0:T(8,128)(2,1)S(1)}, u32[]{:S(2)}, u32[]{:S(2)}) async-start(bf16[8,32,512]{2,1,0:T(8,128)(2,1)} %shard_map.106), calls=%async_computation.6 | async-start | bytes 524288 | tf_op jit(solution)/shard_map/all_to_all | solution.py:51
  113.7 0.0 reduce-scatter.5.cloned.1.call-start
  113.8 0.0 reduce-scatter.3.cloned.1.call-done
  113.8 0.7 reduce-scatter.5.cloned.1.call-update
  114.5 5.0 %collective-permute-start.7 = (bf16[256,512]{1,0:T(8,128)(2,1)}, bf16[256,512]{1,0:T(8,128)(2,1)S(1)}, u32[]{:S(2)}, u32[]{:S(2)}) collective-permute-start(bf16[256,512]{1,0:T(8,128)(2,1)} %copy-done.15), channel_id=1, source_target_pairs={{0,0},{1,4},{2,1},{3,5},{4,2},{5,6},{6,3},{7,7},{8,8},{9,12},{10,9... | collective-permute-start | bytes 786440 | tf_op jit(solution)/shard_map/ppermute | solution.py:47
  119.5 1.6 %collective-permute-start.8 = (bf16[256,512]{1,0:T(8,128)(2,1)}, bf16[256,512]{1,0:T(8,128)(2,1)S(1)}, u32[]{:S(2)}, u32[]{:S(2)}) collective-permute-start(bf16[256,512]{1,0:T(8,128)(2,1)} %copy-done.14), channel_id=1, source_target_pairs={{0,4},{1,1},{2,5},{3,0},{4,6},{5,3},{6,7},{7,2},{8,12},{9,9},{10,1... | collective-permute-start | bytes 786440 | tf_op jit(solution)/shard_map/ppermute | solution.py:47
  121.1 0.0 collective-permute-start.9
  121.1 4.0 %collective-permute-start.10 = (bf16[256,512]{1,0:T(8,128)(2,1)}, bf16[256,512]{1,0:T(8,128)(2,1)S(1)}, u32[]{:S(2)}, u32[]{:S(2)}) collective-permute-start(bf16[256,512]{1,0:T(8,128)(2,1)} %copy-done.12), channel_id=1, source_target_pairs={{0,5},{1,0},{2,4},{3,1},{4,7},{5,2},{6,6},{7,3},{8,13},{9,8},{10,1... | collective-permute-start | bytes 786440 | tf_op jit(solution)/shard_map/ppermute | solution.py:47
  125.2 1.4 collective-permute-done.7.a0
  126.5 0.0 collective-permute-done.8.a1
  126.5 3.4 %collective-permute-done.9.a2 = bf16[256,512]{1,0:T(8,128)(2,1)S(1)} collective-permute-done((bf16[256,512]{1,0:T(8,128)(2,1)}, bf16[256,512]{1,0:T(8,128)(2,1)S(1)}, u32[]{:S(2)}, u32[]{:S(2)}) %collective-permute-start.9) | collective-permute-done | bytes 262176 | tf_op jit(solution)/shard_map/ppermute | solution.py:47
  130.0 1.8 %collective-permute-done.10.a3 = bf16[256,512]{1,0:T(8,128)(2,1)S(1)} collective-permute-done((bf16[256,512]{1,0:T(8,128)(2,1)}, bf16[256,512]{1,0:T(8,128)(2,1)S(1)}, u32[]{:S(2)}, u32[]{:S(2)}) %collective-permute-start.10) | collective-permute-done | bytes 262176 | tf_op jit(solution)/shard_map/ppermute | solution.py:47
  131.8 0.9 copy-done.1
  132.7 2.8 %shard_map.105 = (bf16[256,512]{1,0:T(8,128)(2,1)}, bf16[256,128]{1,0:T(8,128)(2,1)}, bf16[256,128]{1,0:T(8,128)(2,1)}) custom-call(s32[2]{0:T(128)S(1)} %pad_add_fusion.place._, bf16[256,512]{1,0:T(8,128)(2,1)S(1)} %collective-permute-done.7.a0, bf16[256,512]{1,0:T(8,128)(2,1)S(1)} %collective-permute-done.8.a1, ...), custom_call_target="tpu_custom_call" | custom-call | flops 335544320 | bytes 3145728 | tf_op jit(solution)/shard_map/pallas_call | solution.py:73
  135.6 6.5 %reduce-scatter.5.cloned.1.call-done.first = bf16[48,512]{1,0:T(8,128)(2,1)} async-done(((bf16[192,512]{1,0:T(8,128)(2,1)}), bf16[48,512]{1,0:T(8,128)(2,1)}) %reduce-scatter.5.cloned.1.call-update) | async-done | bytes 49168 | tf_op jit(solution)/shard_map/reduce_scatter | solution.py:59
  142.1 0.8 copy-done.6
  142.9 0.6 shard_map.107
  143.5 1.9 %collective-permute-start.11 = (bf16[80,512]{1,0:T(8,128)(2,1)S(1)}, bf16[80,512]{1,0:T(8,128)(2,1)S(1)}, u32[]{:S(2)}, u32[]{:S(2)}) collective-permute-start(bf16[80,512]{1,0:T(8,128)(2,1)S(1)} %shard_map.107), channel_id=1, source_target_pairs={{0,0},{1,64},{2,128},{3,192},{4,2},{5,66},{6,130},{7,194},{8,8},{9... | collective-permute-start | bytes 245768 | tf_op jit(solution)/shard_map/ppermute | solution.py:47
  145.4 0.0 collective-permute-done.6
  145.4 2.1 %add_convert_fusion = bf16[256,1280]{1,0:T(8,128)(2,1)} fusion(f32[256,1280]{1,0:T(8,128)S(1)} %get-tuple-element.23, bf16[256,1280]{1,0:T(8,128)(2,1)} %collective-permute-done.6), kind=kLoop, calls=%fused_computation | loop fusion | flops 983040 | bytes 2621440 | tf_op jit(solution)/shard_map/convert_element_type | solution.py:241
  147.5 4.9 %collective-permute-done.11 = bf16[80,512]{1,0:T(8,128)(2,1)S(1)} collective-permute-done((bf16[80,512]{1,0:T(8,128)(2,1)S(1)}, bf16[80,512]{1,0:T(8,128)(2,1)S(1)}, u32[]{:S(2)}, u32[]{:S(2)}) %collective-permute-start.11) | collective-permute-done | bytes 81952 | tf_op jit(solution)/shard_map/ppermute | solution.py:47
  152.4 0.7 convert_bitcast_fusion
  (29 shorter events, 0.1 us)
Async XLA Ops:
  7.2 45.4 %copy-start.8 = (bf16[256,1280]{1,0:T(8,128)(2,1)S(1)}, bf16[256,1280]{1,0:T(8,128)(2,1)}, u32[]{:S(2)}) copy-start(bf16[256,1280]{1,0:T(8,128)(2,1)} %own.3) | copy-start | bytes 1966084
  7.2 88.4 %all-gather.2.cloned.1.call-start = ((), (), s32[]{:S(2)}) async-start(), calls=%async_computation.7 | async-start | bytes 1769472 | tf_op jit(solution)/shard_map/all_gather | solution.py:55
  7.2 7.6 %collective-permute-start.5 = (bf16[80,512]{1,0:T(8,128)(2,1)}, bf16[80,512]{1,0:T(8,128)(2,1)S(1)}, u32[]{:S(2)}, u32[]{:S(2)}) collective-permute-start(bf16[80,512]{1,0:T(8,128)(2,1)} %bitcast.12), channel_id=1, source_target_pairs={{0,0},{1,128},{2,4},{3,132},{4,64},{5,192},{6,68},{7,196},{8,8},{9... | collective-permute-start | bytes 245768 | tf_op jit(solution)/shard_map/ppermute | solution.py:47
  25.8 88.0 %reduce-scatter.3.cloned.1.call-start = ((), (), s32[]{:S(2)}) async-start(), calls=%async_computation.8 | async-start | bytes 1769472 | tf_op jit(solution)/shard_map/reduce_scatter | solution.py:59
  25.8 26.7 %collective-permute-start = (bf16[256,1280]{1,0:T(8,128)(2,1)}, bf16[256,1280]{1,0:T(8,128)(2,1)S(1)}, u32[]{:S(2)}, u32[]{:S(2)}) collective-permute-start(bf16[256,1280]{1,0:T(8,128)(2,1)} %own.3), channel_id=1, source_target_pairs={{0,4},{1,5},{2,6},{3,7},{4,0},{5,1},{6,2},{7,3},{8,12},{9,13},{10,... | collective-permute-start | bytes 1966088 | tf_op jit(solution)/shard_map/ppermute | solution.py:47
  26.3 0.9 copy-start
  27.2 0.8 copy-start.2
  28.0 0.8 copy-start.4
  28.9 0.7 copy-start.16
  31.2 10.8 %collective-permute-start.4 = (bf16[256,512]{1,0:T(8,128)(2,1)S(1)}, bf16[256,512]{1,0:T(8,128)(2,1)S(1)}, u32[]{:S(2)}, u32[]{:S(2)}) collective-permute-start(bf16[256,512]{1,0:T(8,128)(2,1)S(1)} %get-tuple-element.20), channel_id=1, source_target_pairs={{0,3},{1,1},{2,7},{3,5},{4,0},{5,2},{6,4},{7,6},{8,11},{9,9},{10,1... | collective-permute-start | bytes 786440 | tf_op jit(solution)/shard_map/ppermute | solution.py:47
  31.9 10.1 %collective-permute-start.3 = (bf16[256,512]{1,0:T(8,128)(2,1)S(1)}, bf16[256,512]{1,0:T(8,128)(2,1)S(1)}, u32[]{:S(2)}, u32[]{:S(2)}) collective-permute-start(bf16[256,512]{1,0:T(8,128)(2,1)S(1)} %get-tuple-element.20), channel_id=1, source_target_pairs={{0,2},{1,0},{2,6},{3,4},{4,3},{5,1},{6,7},{7,5},{8,10},{9,8},{10,1... | collective-permute-start | bytes 786440 | tf_op jit(solution)/shard_map/ppermute | solution.py:47
  38.1 13.0 %collective-permute-start.2 = (bf16[256,512]{1,0:T(8,128)(2,1)S(1)}, bf16[256,512]{1,0:T(8,128)(2,1)S(1)}, u32[]{:S(2)}, u32[]{:S(2)}) collective-permute-start(bf16[256,512]{1,0:T(8,128)(2,1)S(1)} %get-tuple-element.20), channel_id=1, source_target_pairs={{0,1},{1,3},{2,5},{3,7},{4,2},{5,0},{6,6},{7,4},{8,9},{9,11},{10,1... | collective-permute-start | bytes 786440 | tf_op jit(solution)/shard_map/ppermute | solution.py:47
  40.0 12.5 %collective-permute-start.1 = (bf16[256,512]{1,0:T(8,128)(2,1)S(1)}, bf16[256,512]{1,0:T(8,128)(2,1)}, u32[]{:S(2)}, u32[]{:S(2)}) collective-permute-start(bf16[256,512]{1,0:T(8,128)(2,1)S(1)} %get-tuple-element.20), channel_id=1, source_target_pairs={{0,0},{1,2},{2,4},{3,6},{4,1},{5,3},{6,5},{7,7},{8,8},{9,10},{10,1... | collective-permute-start | bytes 786440 | tf_op jit(solution)/shard_map/ppermute | solution.py:47
  52.5 4.4 %copy-start.10 = (bf16[256,1280]{1,0:T(8,128)(2,1)}, bf16[256,1280]{1,0:T(8,128)(2,1)S(1)}, u32[]{:S(2)}) copy-start(bf16[256,1280]{1,0:T(8,128)(2,1)S(1)} %collective-permute-done.other) | copy-start | bytes 1966084
  57.0 1.0 copy-start.17
  92.0 14.8 %all-to-all-start.3 = ((bf16[4,8,32,512]{3,2,1,0:T(8,128)(2,1)}), bf16[4,8,32,512]{3,2,1,0:T(8,128)(2,1)S(1)}, u32[]{:S(2)}, u32[]{:S(2)}) async-start(bf16[4,8,32,512]{3,2,1,0:T(8,128)(2,1)} %get-tuple-element.34), calls=%async_computation.5 | async-start | bytes 2097152 | tf_op jit(solution)/shard_map/all_to_all | solution.py:51
  95.6 1.4 copy-start.7
  97.0 1.1 copy-start.9
  98.1 1.1 copy-start.11
  99.2 3.0 %copy-start.18 = (bf16[512,1024]{1,0:T(8,128)(2,1)S(1)}, bf16[512,1024]{1,0:T(8,128)(2,1)}, u32[]{:S(2)}) copy-start(bf16[512,1024]{1,0:T(8,128)(2,1)} %copy-done.17) | copy-start | bytes 3145732
  101.5 0.7 copy-start.15
  102.2 3.0 %copy-start.12 = (bf16[256,512]{1,0:T(8,128)(2,1)}, bf16[256,512]{1,0:T(8,128)(2,1)S(1)}, u32[]{:S(2)}) copy-start(bf16[256,512]{1,0:T(8,128)(2,1)S(1)} %get-tuple-element.28) | copy-start | bytes 786436
  102.2 3.0 %copy-start.13 = (bf16[256,512]{1,0:T(8,128)(2,1)}, bf16[256,512]{1,0:T(8,128)(2,1)S(1)}, u32[]{:S(2)}) copy-start(bf16[256,512]{1,0:T(8,128)(2,1)S(1)} %get-tuple-element.27) | copy-start | bytes 786436
  102.2 3.0 %copy-start.14 = (bf16[256,512]{1,0:T(8,128)(2,1)}, bf16[256,512]{1,0:T(8,128)(2,1)S(1)}, u32[]{:S(2)}) copy-start(bf16[256,512]{1,0:T(8,128)(2,1)S(1)} %get-tuple-element.26) | copy-start | bytes 786436
  105.2 26.6 %copy-start.3 = (bf16[256,128]{1,0:T(8,128)(2,1)S(1)}, bf16[256,128]{1,0:T(8,128)(2,1)}, u32[]{:S(2)}) copy-start(bf16[256,128]{1,0:T(8,128)(2,1)} %k_ref.3) | copy-start | bytes 196612
  105.2 26.6 %copy-start.5 = (bf16[256,128]{1,0:T(8,128)(2,1)S(1)}, bf16[256,128]{1,0:T(8,128)(2,1)}, u32[]{:S(2)}) copy-start(bf16[256,128]{1,0:T(8,128)(2,1)} %v_ref.3) | copy-start | bytes 196612
  105.2 40.2 %collective-permute-start.6 = (bf16[256,1280]{1,0:T(8,128)(2,1)}, bf16[256,1280]{1,0:T(8,128)(2,1)}, u32[]{:S(2)}, u32[]{:S(2)}) collective-permute-start(bf16[256,1280]{1,0:T(8,128)(2,1)} %get-tuple-element.24), channel_id=1, source_target_pairs={{0,4},{1,5},{2,6},{3,7},{4,0},{5,1},{6,2},{7,3},{8,12},{9,13},{10,... | collective-permute-start | bytes 1966088 | tf_op jit(solution)/shard_map/ppermute | solution.py:47
  108.2 27.4 %all-to-all-start.4 = ((bf16[8,32,512]{2,1,0:T(8,128)(2,1)}), bf16[8,32,512]{2,1,0:T(8,128)(2,1)S(1)}, u32[]{:S(2)}, u32[]{:S(2)}) async-start(bf16[8,32,512]{2,1,0:T(8,128)(2,1)} %shard_map.106), calls=%async_computation.6 | async-start | bytes 524288 | tf_op jit(solution)/shard_map/all_to_all | solution.py:51
  113.7 28.3 %reduce-scatter.5.cloned.1.call-start = ((), (), s32[]{:S(2)}) async-start(), calls=%async_computation.9 | async-start | bytes 245760 | tf_op jit(solution)/shard_map/reduce_scatter | solution.py:59
  114.5 12.0 %collective-permute-start.7 = (bf16[256,512]{1,0:T(8,128)(2,1)}, bf16[256,512]{1,0:T(8,128)(2,1)S(1)}, u32[]{:S(2)}, u32[]{:S(2)}) collective-permute-start(bf16[256,512]{1,0:T(8,128)(2,1)} %copy-done.15), channel_id=1, source_target_pairs={{0,0},{1,4},{2,1},{3,5},{4,2},{5,6},{6,3},{7,7},{8,8},{9,12},{10,9... | collective-permute-start | bytes 786440 | tf_op jit(solution)/shard_map/ppermute | solution.py:47
  119.5 7.0 %collective-permute-start.8 = (bf16[256,512]{1,0:T(8,128)(2,1)}, bf16[256,512]{1,0:T(8,128)(2,1)S(1)}, u32[]{:S(2)}, u32[]{:S(2)}) collective-permute-start(bf16[256,512]{1,0:T(8,128)(2,1)} %copy-done.14), channel_id=1, source_target_pairs={{0,4},{1,1},{2,5},{3,0},{4,6},{5,3},{6,7},{7,2},{8,12},{9,9},{10,1... | collective-permute-start | bytes 786440 | tf_op jit(solution)/shard_map/ppermute | solution.py:47
  121.1 8.8 %collective-permute-start.9 = (bf16[256,512]{1,0:T(8,128)(2,1)}, bf16[256,512]{1,0:T(8,128)(2,1)S(1)}, u32[]{:S(2)}, u32[]{:S(2)}) collective-permute-start(bf16[256,512]{1,0:T(8,128)(2,1)} %copy-done.13), channel_id=1, source_target_pairs={{0,1},{1,5},{2,0},{3,4},{4,3},{5,7},{6,2},{7,6},{8,9},{9,13},{10,8... | collective-permute-start | bytes 786440 | tf_op jit(solution)/shard_map/ppermute | solution.py:47
  121.1 10.6 %collective-permute-start.10 = (bf16[256,512]{1,0:T(8,128)(2,1)}, bf16[256,512]{1,0:T(8,128)(2,1)S(1)}, u32[]{:S(2)}, u32[]{:S(2)}) collective-permute-start(bf16[256,512]{1,0:T(8,128)(2,1)} %copy-done.12), channel_id=1, source_target_pairs={{0,5},{1,0},{2,4},{3,1},{4,7},{5,2},{6,6},{7,3},{8,13},{9,8},{10,1... | collective-permute-start | bytes 786440 | tf_op jit(solution)/shard_map/ppermute | solution.py:47
  131.8 1.0 copy-start.1
  142.1 0.8 copy-start.6
  143.5 8.9 %collective-permute-start.11 = (bf16[80,512]{1,0:T(8,128)(2,1)S(1)}, bf16[80,512]{1,0:T(8,128)(2,1)S(1)}, u32[]{:S(2)}, u32[]{:S(2)}) collective-permute-start(bf16[80,512]{1,0:T(8,128)(2,1)S(1)} %shard_map.107), channel_id=1, source_target_pairs={{0,0},{1,64},{2,128},{3,192},{4,2},{5,66},{6,130},{7,194},{8,8},{9... | collective-permute-start | bytes 245768 | tf_op jit(solution)/shard_map/ppermute | solution.py:47
Sparse Core Ops, SparseCore 0:
  25.9 42.1 all-gather.1
  70.6 41.7 reduce-scatter.2
  117.1 24.9 reduce-scatter.4

commit v3 on v2

--- a/solution.py
+++ b/solution.py
@@ -13,8 +13,6 @@
 GROUP = HEADS * HEAD
 COLS = 1280
 SHARD = 80
-FIRST = 48
-REST = SHARD - FIRST
 AXES = ("dp", "mp")
 BF, F32 = jnp.bfloat16, jnp.float32
 SCALE = HEAD ** -0.5
@@ -51,10 +49,6 @@
     return lax.all_to_all(blocks, "dp", 0, 0, axis_index_groups=groups, tiled=True)
 
 
-def gather(block, groups):
-    return lax.all_gather(block, "dp", axis_index_groups=groups, tiled=True)
-
-
 def scatter(blocks, groups):
     return lax.psum_scatter(blocks, "dp", axis_index_groups=groups, tiled=True)
 
@@ -67,16 +61,21 @@
     return lax.dot_general(a, b, (dims, ((), ())), preferred_element_type=F32)
 
 
-def call(body, outs, scratch=(), flops=0, moved=0):
+def whole(array):
+    dims = array.shape
+    return pl.BlockSpec(dims, lambda i: (0,) * len(dims), pipeline_mode=pl.Buffered(1))
+
+
+def call(body, outs, scratch=(), flops=0, moved=0, limit=40):
     def run(scalars, *operands):
-        vmem = pl.BlockSpec(memory_space=pltpu.VMEM)
         return pl.pallas_call(
             body,
             out_shape=outs,
-            in_specs=[pl.BlockSpec(memory_space=pltpu.SMEM)] + [vmem] * len(operands),
-            out_specs=jax.tree.map(lambda _: vmem, outs),
+            grid=(1,),
+            in_specs=[pl.BlockSpec(memory_space=pltpu.SMEM)] + [whole(a) for a in operands],
+            out_specs=jax.tree.map(whole, outs),
             scratch_shapes=list(scratch),
-            compiler_params=pltpu.CompilerParams(vmem_limit_bytes=40 << 20),
+            compiler_params=pltpu.CompilerParams(vmem_limit_bytes=limit << 20),
             cost_estimate=pl.CostEstimate(flops=flops, bytes_accessed=moved, transcendentals=0),
         )(scalars, *operands)
 
@@ -130,7 +129,7 @@
     dv_ref[...] = value_sum.astype(BF)
 
 
-def weight_grad_body(place, own, other, r0, r1, r2, r3, first_ref, rest_ref, att_ref, og, total):
+def weight_grad_body(place, own, other, r0, r1, r2, r3, grad_ref, att_ref, og):
     c, y = place[0], place[1]
     og[pl.ds(pl.multiple_of(c * TOK, TOK), TOK), :] = own[...]
     og[pl.ds(pl.multiple_of((1 - c) * TOK, TOK), TOK), :] = other[...]
@@ -141,27 +140,19 @@
             pl.ds(pl.multiple_of((j // 2) * GROUP, GROUP), GROUP),
         ] = ref[...]
     for i in range(COLS // 256):
-        total[i * 256 : (i + 1) * 256, :] = dot(
+        grad_ref[i * 256 : (i + 1) * 256, :] = dot(
             og[:, i * 256 : (i + 1) * 256], att_ref[...], ((0,), (0,))
         ).astype(BF)
-    for z in range(NZ):
-        for j in range(4):
-            base = z * 160 + (j % 2) * SHARD
-            lanes = slice((j // 2) * GROUP, (j // 2 + 1) * GROUP)
-            first_ref[z, j] = total[base : base + FIRST, lanes]
-            rest_ref[j, z] = total[base + FIRST : base + SHARD, lanes]
-
-
-def attn_grad_body(place, own, other, first, rest, g0, g1, g2, g3, wt_ref, og):
+
+
+def attn_grad_body(place, own, other, blocks, g0, g1, g2, g3, wt_ref, og):
     c, y = place[0], place[1]
     og[pl.ds(pl.multiple_of(c * TOK, TOK), TOK), :] = own[...]
     og[pl.ds(pl.multiple_of((1 - c) * TOK, TOK), TOK), :] = other[...]
     for z in range(NZ):
         for j in range(4):
             base = z * 160 + (j % 2) * SHARD
-            lanes = slice((j // 2) * GROUP, (j // 2 + 1) * GROUP)
-            wt_ref[base : base + FIRST, lanes] = first[z, j]
-            wt_ref[base + FIRST : base + SHARD, lanes] = rest[j, z]
+            wt_ref[base : base + SHARD, (j // 2) * GROUP : (j // 2 + 1) * GROUP] = blocks[j, z]
     for k, ref in enumerate((g0, g1, g2, g3)):
         m = (y + k) % 4
         ref[...] = dot(
@@ -180,27 +171,22 @@
 
 
 def sum_x_body(_, blocks, out):
-    for z in range(NZ):
-        out[z] = (
-            (blocks[0, z].astype(F32) + blocks[1, z].astype(F32))
-            + (blocks[2, z].astype(F32) + blocks[3, z].astype(F32))
-        ).astype(BF)
-
-
-def sum_z_body(_, first, blocks, out):
-    out[:FIRST, :] = first[...]
-    total = blocks[0].astype(F32)
-    for z in range(1, NZ):
-        total = total + blocks[z].astype(F32)
-    out[FIRST:, :] = total.astype(BF)
+    out[...] = (
+        (blocks[0].astype(F32) + blocks[1].astype(F32))
+        + (blocks[2].astype(F32) + blocks[3].astype(F32))
+    ).astype(BF)
+
+
+def split_body(_, rows, out):
+    for j in range(4):
+        out[j] = rows[(j % 2) * SHARD : (j % 2 + 1) * SHARD, (j // 2) * GROUP : (j // 2 + 1) * GROUP]
 
 
 def per_device(query_rows, key_rows, value_matrix, out_weight, out_grad, doc_lengths):
     dp, y = lax.axis_index("dp"), lax.axis_index("mp")
     place = jnp.stack([dp % NC, y]).astype(jnp.int32)
     wt = send(out_weight.T, TO_PLANE)
-    rest_w = to_all(to_all(wt[FIRST:], Z_GROUPS), X_GROUPS)
-    first_w = gather(to_all(wt[:FIRST], X_GROUPS).reshape(-1, GROUP), Z_GROUPS)
+    blocks = to_all(to_all(wt, Z_GROUPS), X_GROUPS)
     other_grad = send(out_grad, SWAP)
 
     attended, prob = call(
@@ -208,17 +194,19 @@
         (shape(TOK, GROUP), shape(HEADS, TOK, TOK, dtype=F32)),
         flops=4 * 4 * TOK * TOK * HEAD,
         moved=2 << 20,
+        limit=63,
     )(doc_lengths[0], query_rows, key_rows, value_matrix)
     heads = [send(attended, pairs) for pairs in HEADS_OUT]
 
     big = 2 * 2 * TOK * COLS * 2 * GROUP
-    first_part, rest_part, attended_two = call(
+    grad_part, attended_two = call(
         weight_grad_body,
-        (shape(NZ, 4, FIRST, GROUP), shape(4, NZ, REST, GROUP), shape(2 * TOK, 2 * GROUP)),
-        scratch=(pltpu.VMEM((2 * TOK, COLS), BF), pltpu.VMEM((COLS, 2 * GROUP), BF)),
+        (shape(COLS, 2 * GROUP), shape(2 * TOK, 2 * GROUP)),
+        scratch=(pltpu.VMEM((2 * TOK, COLS), BF),),
         flops=big,
         moved=8 << 20,
     )(place, out_grad, other_grad, *heads)
+    grad_rows = scatter(grad_part, Z_GROUPS)
 
     *partials, wt_two = call(
         attn_grad_body,
@@ -226,26 +214,19 @@
         scratch=(pltpu.VMEM((2 * TOK, COLS), BF),),
         flops=big,
         moved=8 << 20,
-    )(
-        place,
-        out_grad,
-        other_grad,
-        first_w.reshape(NZ, 4, FIRST, GROUP),
-        rest_w.reshape(4, NZ, REST, GROUP),
-    )
+    )(place, out_grad, other_grad, blocks)
     upstream = [send(partial, pairs) for partial, pairs in zip(partials, HEADS_BACK)]
 
     mine, theirs = call(
         layer_out_body, (shape(TOK, COLS, dtype=F32), shape(TOK, COLS)), flops=big, moved=6 << 20
     )(place, attended_two, wt_two)
-    layer_out = (mine + send(theirs, SWAP).astype(F32)).astype(BF)
-
-    first_sum = scatter(scatter(first_part.reshape(-1, GROUP), Z_GROUPS), X_GROUPS)
-    rest_sum = call(sum_x_body, shape(NZ, REST, GROUP), moved=2 << 20)(
-        place, exchange(rest_part, X_GROUPS)
+    theirs = send(theirs, SWAP)
+    layer_out = (mine + theirs.astype(F32)).astype(BF)
+
+    pieces = call(split_body, shape(4, SHARD, GROUP), moved=1 << 20)(place, grad_rows)
+    weight_grad = call(sum_x_body, shape(SHARD, GROUP), moved=1 << 20)(
+        place, exchange(pieces, X_GROUPS)
     )
-    rest_sum = exchange(rest_sum, Z_GROUPS)
-    weight_grad = call(sum_z_body, shape(SHARD, GROUP), moved=1 << 20)(place, first_sum, rest_sum)
     weight_grad = send(weight_grad, TO_OWNER).astype(F32)
 
     query_grad, key_grad, value_grad = call(
@@ -253,6 +234,7 @@
         (shape(TOK, GROUP), shape(TOK, HEAD), shape(TOK, HEAD)),
         flops=5 * 4 * 2 * TOK * TOK * HEAD,
         moved=3 << 20,
+        limit=63,
     )(place, *upstream, query_rows, key_rows, value_matrix, prob)
     return (layer_out, query_grad, key_grad, value_grad, weight_grad.T)
 

time: 161 us -> 165 us (1.025)
  blocking collectives: 44.8 us -> 72.6 us
  waiting for transfers between devices: 33.4 us -> 16.7 us
  local copies, waits for them, and re-layouts: 10.5 us -> 4.22 us
  starting transfers between devices: 38 us -> 33 us
  Pallas kernels: 16.1 us -> 19.1 us
    all_to_all x3 -> x2, blocking collectives: 44.8 us -> 72.6 us  [exchange(): lax.all_to_all(blocks, 'dp', 0, 0, axis_index_groups=groups, tiled=True)]
    ppermute x12, waiting for transfers between devices: 24.6 us -> 16.7 us  [send(): return lax.ppermute(value, AXES, pairs)]
    reduce_scatter x2 -> x1, waiting for transfers between devices: 6.56 us -> 0.01 us  [scatter(): return lax.psum_scatter(blocks, 'dp', axis_index_groups=groups, tiled=True)]
    unnamed x38 -> x22, local copies, waits for them, and re-layouts: 10.4 us -> 3.88 us
    all_to_all x2 -> x1, starting transfers between devices: 9.08 us -> 3.58 us  [exchange(): lax.all_to_all(blocks, 'dp', 0, 0, axis_index_groups=groups, tiled=True)]
    pallas_call x7, Pallas kernels: 16.1 us -> 19.1 us  [run(): pl.pallas_call(body, out_shape=outs, grid=(1,), in_specs=[pl.BlockSpec(me...]
  transfers between devices with their start and end apart: 17 -> 14, of which waited for: 9 -> 5; matrix products, arithmetic and copies ran while one was open for 1% -> 2% of each run, Pallas kernels for 10% -> 9%
where the time goes in v3:
time: 165 us; the launch traced here: 163 us
  blocking collectives  72.6 us (44%)
  starting transfers between devices  33 us (20%)
  Pallas kernels  19.1 us (12%)
  waiting for transfers between devices  16.7 us (10%)
  between operations  14.2 us (9%)
  local copies, waits for them, and re-layouts  4.22 us (3%)
  other arithmetic  3.19 us (2%)
    all_to_all x2, blocking collectives, exchange(): lax.all_to_all(blocks, 'dp', 0, 0, axis_index_groups=groups, tiled=True)  72.6 us
    ppermute x12, starting transfers between devices, send(): return lax.ppermute(value, AXES, pairs)  29.3 us
    pallas_call x7, Pallas kernels, run(): pl.pallas_call(body, out_shape=outs, grid=(1,), in_specs=[pl.BlockSpec(me...  19.1 us
    ppermute x12, waiting for transfers between devices, send(): return lax.ppermute(value, AXES, pairs)  16.7 us
    unnamed x22, local copies, waits for them, and re-layouts  3.88 us
    all_to_all x1, starting transfers between devices, exchange(): lax.all_to_all(blocks, 'dp', 0, 0, axis_index_groups=groups, tiled=True)  3.58 us
  transfers between devices with their start and end apart: 14, of which 5 were waited for; matrix products, arithmetic and copies ran while one was open for 2% of the time, Pallas kernels for 9%

profile of v3, /device:TPU:8, one launch (start us, length us, event | category | flops | bytes accessed | tf_op | source)
XLA Modules:
  0.0 162.9 jit_solution(4301183503462962572)
XLA Ops:
  7.2 0.0 reduce-scatter.2.cloned.1.call-start
  7.2 0.1 collective-permute-start
  7.3 3.1 %shard_map.101 = (bf16[256,512]{1,0:T(8,128)(2,1)}, f32[4,256,256]{2,1,0:T(8,128)}) custom-call(s32[8]{0:T(128)} %bitcast.7, bf16[256,512]{1,0:T(8,128)(2,1)} %q_ref.3, bf16[256,128]{1,0:T(8,128)(2,1)} %k_ref.3, bf16[256,128]{1,0:T(8,128)(2,1)} %v_ref.3), custom_call_target="tpu_custom_call" | custom-call | flops 134217728 | bytes 2097152 | tf_op jit(solution)/shard_map/pallas_call | solution.py:71
  10.4 3.5 %collective-permute-start.1 = (bf16[256,512]{1,0:T(8,128)(2,1)}, bf16[256,512]{1,0:T(8,128)(2,1)S(1)}, u32[]{:S(2)}, u32[]{:S(2)}) collective-permute-start(bf16[256,512]{1,0:T(8,128)(2,1)} %get-tuple-element.19), channel_id=1, source_target_pairs={{0,0},{1,2},{2,4},{3,6},{4,1},{5,3},{6,5},{7,7},{8,8},{9,10},{10,1... | collective-permute-start | bytes 786440 | tf_op jit(solution)/shard_map/ppermute | solution.py:45
  13.9 3.5 %collective-permute-start.2 = (bf16[256,512]{1,0:T(8,128)(2,1)}, bf16[256,512]{1,0:T(8,128)(2,1)S(1)}, u32[]{:S(2)}, u32[]{:S(2)}) collective-permute-start(bf16[256,512]{1,0:T(8,128)(2,1)} %get-tuple-element.19), channel_id=1, source_target_pairs={{0,1},{1,3},{2,5},{3,7},{4,2},{5,0},{6,6},{7,4},{8,9},{9,11},{10,1... | collective-permute-start | bytes 786440 | tf_op jit(solution)/shard_map/ppermute | solution.py:45
  17.3 0.6 collective-permute-start.3
  17.9 1.6 collective-permute-start.4
  19.5 0.1 pad_add_fusion.place._
  19.6 0.0 copy-start.2
  19.6 0.0 collective-permute-done.1.r0
  19.6 4.2 %collective-permute-done.2.r1 = bf16[256,512]{1,0:T(8,128)(2,1)S(1)} collective-permute-done((bf16[256,512]{1,0:T(8,128)(2,1)}, bf16[256,512]{1,0:T(8,128)(2,1)S(1)}, u32[]{:S(2)}, u32[]{:S(2)}) %collective-permute-start.2) | collective-permute-done | bytes 262176 | tf_op jit(solution)/shard_map/ppermute | solution.py:45
  23.8 2.8 %collective-permute-done.3.r2 = bf16[256,512]{1,0:T(8,128)(2,1)S(1)} collective-permute-done((bf16[256,512]{1,0:T(8,128)(2,1)}, bf16[256,512]{1,0:T(8,128)(2,1)S(1)}, u32[]{:S(2)}, u32[]{:S(2)}) %collective-permute-start.3) | collective-permute-done | bytes 262176 | tf_op jit(solution)/shard_map/ppermute | solution.py:45
  26.6 0.0 collective-permute-done.4.r3
  26.6 0.0 collective-permute-done.other
  26.6 0.0 copy-start.4
  26.6 1.1 copy-done.4
  27.7 0.0 copy-start.10
  27.7 4.3 %shard_map.102 = (bf16[1280,1024]{1,0:T(8,128)(2,1)}, bf16[512,1024]{1,0:T(8,128)(2,1)S(1)}) custom-call(s32[2]{0:T(128)S(1)} %pad_add_fusion.place._, bf16[256,1280]{1,0:T(8,128)(2,1)S(1)} %copy-done.4, bf16[256,1280]{1,0:T(8,128)(2,1)} %collective-permute-done.other, bf16[256,512]{1,0:T(8,128)(2,1)S(1)} %collective-permute-done.1.r0, ...), custom_call_target="tpu_custom_call" | custom-call | flops 1342177280 | bytes 8388608 | tf_op jit(solution)/shard_map/pallas_call | solution.py:71
  32.1 0.0 reduce-scatter.2.cloned.1.call-update
  32.1 0.0 copy-done.10
  32.1 6.7 %collective-permute-start.5 = (bf16[80,512]{1,0:T(8,128)(2,1)S(1)}, bf16[80,512]{1,0:T(8,128)(2,1)S(1)}, u32[]{:S(2)}, u32[]{:S(2)}) collective-permute-start(bf16[80,512]{1,0:T(8,128)(2,1)S(1)} %bitcast.6), channel_id=1, source_target_pairs={{0,0},{1,128},{2,4},{3,132},{4,64},{5,192},{6,68},{7,196},{8,8},{9... | collective-permute-start | bytes 245768 | tf_op jit(solution)/shard_map/ppermute | solution.py:45
  38.8 2.0 %collective-permute-done.5 = bf16[80,512]{1,0:T(8,128)(2,1)S(1)} collective-permute-done((bf16[80,512]{1,0:T(8,128)(2,1)S(1)}, bf16[80,512]{1,0:T(8,128)(2,1)S(1)}, u32[]{:S(2)}, u32[]{:S(2)}) %collective-permute-start.5) | collective-permute-done | bytes 81952 | tf_op jit(solution)/shard_map/ppermute | solution.py:45
  40.9 36.6 %all_to_all.15 = bf16[8,80,512]{2,1,0:T(8,128)(2,1)S(1)} all-to-all(bf16[8,80,512]{2,1,0:T(8,128)(2,1)S(1)} %broadcast_in_dim.4), channel_id=1, replica_groups={{0,8,16,24,32,40,48,56},{4,12,20,28,36,44,52,60},{64,72,80,88,96,104,11..., dimensions={0} | all-to-all | bytes 1310720 | tf_op jit(solution)/shard_map/all_to_all | solution.py:49
  77.6 0.3 broadcast_in_dim.5
  77.9 0.0 copy-start.5
  77.9 35.9 %all_to_all.16.blocks = bf16[4,8,80,512]{3,2,1,0:T(8,128)(2,1)S(1)} all-to-all(bf16[4,8,80,512]{3,2,1,0:T(8,128)(2,1)S(1)} %broadcast_in_dim.5), channel_id=1, replica_groups={{0,64,128,192},{4,68,132,196},{8,72,136,200},{12,76,140,204},{16,80,144..., dimensions={0} | all-to-all | bytes 5242880 | tf_op jit(solution)/shard_map/all_to_all | solution.py:49
  113.8 0.0 copy-done.5
  113.8 2.9 %shard_map.103 = (bf16[256,512]{1,0:T(8,128)(2,1)S(1)}, bf16[256,512]{1,0:T(8,128)(2,1)S(1)}, bf16[256,512]{1,0:T(8,128)(2,1)S(1)}, bf16[256,512]{1,0:T(8,128)(2,1)S(1)}, bf16[1280,1024]{1,0:T(8,128)(2,1)S(1)}) custom-call(s32[2]{0:T(128)S(1)} %pad_add_fusion.place._, bf16[256,1280]{1,0:T(8,128)(2,1)S(1)} %copy-done.5, ...), custom_call_target="tpu_custom_call" | custom-call | flops 1342177280 | bytes 8388608 | tf_op jit(solution)/shard_map/pallas_call | solution.py:71
  116.7 2.9 %shard_map.104 = (f32[256,1280]{1,0:T(8,128)S(1)}, bf16[256,1280]{1,0:T(8,128)(2,1)}) custom-call(s32[2]{0:T(128)S(1)} %pad_add_fusion.place._, bf16[512,1024]{1,0:T(8,128)(2,1)S(1)} %get-tuple-element.20.att, bf16[1280,1024]{1,0:T(8,128)(2,1)S(1)} %get-tuple-element.21.wt), custom_call_target="tpu_custom_call" | custom-call | flops 1342177280 | bytes 6291456 | tf_op jit(solution)/shard_map/pallas_call | solution.py:71
  119.6 0.0 copy-start
  119.6 1.1 copy-done
  120.7 0.2 collective-permute-start.6
  120.9 4.9 %collective-permute-start.10 = (bf16[256,512]{1,0:T(8,128)(2,1)S(1)}, bf16[256,512]{1,0:T(8,128)(2,1)S(1)}, u32[]{:S(2)}, u32[]{:S(2)}) collective-permute-start(bf16[256,512]{1,0:T(8,128)(2,1)S(1)} %get-tuple-element.27), channel_id=1, source_target_pairs={{0,5},{1,0},{2,4},{3,1},{4,7},{5,2},{6,6},{7,3},{8,13},{9,8},{10,1... | collective-permute-start | bytes 786440 | tf_op jit(solution)/shard_map/ppermute | solution.py:45
  125.8 2.0 %collective-permute-start.7 = (bf16[256,512]{1,0:T(8,128)(2,1)S(1)}, bf16[256,512]{1,0:T(8,128)(2,1)S(1)}, u32[]{:S(2)}, u32[]{:S(2)}) collective-permute-start(bf16[256,512]{1,0:T(8,128)(2,1)S(1)} %get-tuple-element.24), channel_id=1, source_target_pairs={{0,0},{1,4},{2,1},{3,5},{4,2},{5,6},{6,3},{7,7},{8,8},{9,12},{10,9... | collective-permute-start | bytes 786440 | tf_op jit(solution)/shard_map/ppermute | solution.py:45
  127.9 0.7 collective-permute-start.8
  128.6 1.9 %collective-permute-start.9 = (bf16[256,512]{1,0:T(8,128)(2,1)S(1)}, bf16[256,512]{1,0:T(8,128)(2,1)S(1)}, u32[]{:S(2)}, u32[]{:S(2)}) collective-permute-start(bf16[256,512]{1,0:T(8,128)(2,1)S(1)} %get-tuple-element.26), channel_id=1, source_target_pairs={{0,1},{1,5},{2,0},{3,4},{4,3},{5,7},{6,2},{7,6},{8,9},{9,13},{10,8... | collective-permute-start | bytes 786440 | tf_op jit(solution)/shard_map/ppermute | solution.py:45
  130.4 0.0 reduce-scatter.2.cloned.1.call-done.rows
  130.4 0.0 copy-done.2
  130.4 0.0 copy-start.1
  130.4 1.0 copy-done.1
  131.4 1.3 shard_map.106
  132.7 0.0 copy-start.3
  132.7 3.6 %all-to-all-start.2 = ((bf16[4,80,512]{2,1,0:T(8,128)(2,1)}), bf16[4,80,512]{2,1,0:T(8,128)(2,1)S(1)}, u32[]{:S(2)}, u32[]{:S(2)}) async-start(bf16[4,80,512]{2,1,0:T(8,128)(2,1)} %shard_map.106), calls=%async_computation.3 | async-start | bytes 655360 | tf_op jit(solution)/shard_map/all_to_all | solution.py:49
  136.3 0.0 collective-permute-done.10.a3
  136.3 0.0 copy-start.6
  136.3 0.0 collective-permute-done.7.a0
  136.3 0.0 copy-start.7
  136.3 0.0 collective-permute-done.8.a1
  136.3 0.0 copy-start.8
  136.3 4.3 %collective-permute-done.9.a2 = bf16[256,512]{1,0:T(8,128)(2,1)S(1)} collective-permute-done((bf16[256,512]{1,0:T(8,128)(2,1)S(1)}, bf16[256,512]{1,0:T(8,128)(2,1)S(1)}, u32[]{:S(2)}, u32[]{:S(2)}) %collective-permute-start.9) | collective-permute-done | bytes 262176 | tf_op jit(solution)/shard_map/ppermute | solution.py:45
  140.7 0.0 copy-done.8
  140.7 0.0 copy-start.9
  140.7 0.7 copy-done.9
  141.4 0.0 copy-done.6
  141.4 0.0 copy-done.7
  141.4 4.0 %shard_map.105 = (bf16[256,512]{1,0:T(8,128)(2,1)}, bf16[256,128]{1,0:T(8,128)(2,1)}, bf16[256,128]{1,0:T(8,128)(2,1)}) custom-call(s32[2]{0:T(128)} %copy-done.2, bf16[256,512]{1,0:T(8,128)(2,1)} %copy-done.7, bf16[256,512]{1,0:T(8,128)(2,1)} %copy-done.8, bf16[256,512]{1,0:T(8,128)(2,1)} %copy-done.9, bf16[256,512]{1,0:T(8,128)(2,1)} %copy-done.6, ...), custom_call_target="tpu_custom_call" | custom-call | flops 335544320 | bytes 3145728 | tf_op jit(solution)/shard_map/pallas_call | solution.py:71
  145.4 0.0 all-to-all-done.2.blocks
  145.4 0.0 copy-done.3
  145.4 0.6 shard_map.107
  146.0 3.7 %collective-permute-start.11 = (bf16[80,512]{1,0:T(8,128)(2,1)S(1)}, bf16[80,512]{1,0:T(8,128)(2,1)S(1)}, u32[]{:S(2)}, u32[]{:S(2)}) collective-permute-start(bf16[80,512]{1,0:T(8,128)(2,1)S(1)} %shard_map.107), channel_id=1, source_target_pairs={{0,0},{1,64},{2,128},{3,192},{4,2},{5,66},{6,130},{7,194},{8,8},{9... | collective-permute-start | bytes 245768 | tf_op jit(solution)/shard_map/ppermute | solution.py:45
  149.7 0.0 collective-permute-done.6
  149.7 2.4 %add_convert_fusion = bf16[256,1280]{1,0:T(8,128)(2,1)} fusion(f32[256,1280]{1,0:T(8,128)} %copy-done, bf16[256,1280]{1,0:T(8,128)(2,1)} %collective-permute-done.6), kind=kLoop, calls=%fused_computation | loop fusion | flops 983040 | bytes 2621440 | tf_op jit(solution)/shard_map/convert_element_type | solution.py:224
  152.2 3.2 %collective-permute-done.11 = bf16[80,512]{1,0:T(8,128)(2,1)S(1)} collective-permute-done((bf16[80,512]{1,0:T(8,128)(2,1)S(1)}, bf16[80,512]{1,0:T(8,128)(2,1)S(1)}, u32[]{:S(2)}, u32[]{:S(2)}) %collective-permute-start.11) | collective-permute-done | bytes 81952 | tf_op jit(solution)/shard_map/ppermute | solution.py:45
  155.4 0.7 convert_bitcast_fusion
  (1 shorter events, 0.0 us)
Async XLA Ops:
  7.2 123.3 %reduce-scatter.2.cloned.1.call-start = ((), (), s32[]{:S(2)}) async-start(), calls=%async_computation.4 | async-start | bytes 2949120 | tf_op jit(solution)/shard_map/reduce_scatter | solution.py:53
  7.2 19.4 %collective-permute-start = (bf16[256,1280]{1,0:T(8,128)(2,1)}, bf16[256,1280]{1,0:T(8,128)(2,1)}, u32[]{:S(2)}, u32[]{:S(2)}) collective-permute-start(bf16[256,1280]{1,0:T(8,128)(2,1)} %own.3), channel_id=1, source_target_pairs={{0,4},{1,5},{2,6},{3,7},{4,0},{5,1},{6,2},{7,3},{8,12},{9,13},{10,... | collective-permute-start | bytes 1966088 | tf_op jit(solution)/shard_map/ppermute | solution.py:45
  10.4 9.2 %collective-permute-start.1 = (bf16[256,512]{1,0:T(8,128)(2,1)}, bf16[256,512]{1,0:T(8,128)(2,1)S(1)}, u32[]{:S(2)}, u32[]{:S(2)}) collective-permute-start(bf16[256,512]{1,0:T(8,128)(2,1)} %get-tuple-element.19), channel_id=1, source_target_pairs={{0,0},{1,2},{2,4},{3,6},{4,1},{5,3},{6,5},{7,7},{8,8},{9,10},{10,1... | collective-permute-start | bytes 786440 | tf_op jit(solution)/shard_map/ppermute | solution.py:45
  13.9 9.9 %collective-permute-start.2 = (bf16[256,512]{1,0:T(8,128)(2,1)}, bf16[256,512]{1,0:T(8,128)(2,1)S(1)}, u32[]{:S(2)}, u32[]{:S(2)}) collective-permute-start(bf16[256,512]{1,0:T(8,128)(2,1)} %get-tuple-element.19), channel_id=1, source_target_pairs={{0,1},{1,3},{2,5},{3,7},{4,2},{5,0},{6,6},{7,4},{8,9},{9,11},{10,1... | collective-permute-start | bytes 786440 | tf_op jit(solution)/shard_map/ppermute | solution.py:45
  17.3 9.3 %collective-permute-start.3 = (bf16[256,512]{1,0:T(8,128)(2,1)}, bf16[256,512]{1,0:T(8,128)(2,1)S(1)}, u32[]{:S(2)}, u32[]{:S(2)}) collective-permute-start(bf16[256,512]{1,0:T(8,128)(2,1)} %get-tuple-element.19), channel_id=1, source_target_pairs={{0,2},{1,0},{2,6},{3,4},{4,3},{5,1},{6,7},{7,5},{8,10},{9,8},{10,1... | collective-permute-start | bytes 786440 | tf_op jit(solution)/shard_map/ppermute | solution.py:45
  17.9 8.7 %collective-permute-start.4 = (bf16[256,512]{1,0:T(8,128)(2,1)}, bf16[256,512]{1,0:T(8,128)(2,1)S(1)}, u32[]{:S(2)}, u32[]{:S(2)}) collective-permute-start(bf16[256,512]{1,0:T(8,128)(2,1)} %get-tuple-element.19), channel_id=1, source_target_pairs={{0,3},{1,1},{2,7},{3,5},{4,0},{5,2},{6,4},{7,6},{8,11},{9,9},{10,1... | collective-permute-start | bytes 786440 | tf_op jit(solution)/shard_map/ppermute | solution.py:45
  19.6 110.9 %copy-start.2 = (s32[2]{0:T(128)}, s32[2]{0:T(128)S(1)}, u32[]{:S(2)}) copy-start(s32[2]{0:T(128)S(1)} %pad_add_fusion.place._) | copy-start | bytes 28
  26.6 1.1 copy-start.4
  27.7 4.4 %copy-start.10 = (bf16[512,80]{0,1:T(8,128)(2,1)S(1)}, bf16[512,80]{0,1:T(8,128)(2,1)}, u32[]{:S(2)}) copy-start(bf16[512,80]{0,1:T(8,128)(2,1)} %param.9) | copy-start | bytes 245764
  32.1 8.8 %collective-permute-start.5 = (bf16[80,512]{1,0:T(8,128)(2,1)S(1)}, bf16[80,512]{1,0:T(8,128)(2,1)S(1)}, u32[]{:S(2)}, u32[]{:S(2)}) collective-permute-start(bf16[80,512]{1,0:T(8,128)(2,1)S(1)} %bitcast.6), channel_id=1, source_target_pairs={{0,0},{1,128},{2,4},{3,132},{4,64},{5,192},{6,68},{7,196},{8,8},{9... | collective-permute-start | bytes 245768 | tf_op jit(solution)/shard_map/ppermute | solution.py:45
  77.9 36.0 %copy-start.5 = (bf16[256,1280]{1,0:T(8,128)(2,1)S(1)}, bf16[256,1280]{1,0:T(8,128)(2,1)}, u32[]{:S(2)}) copy-start(bf16[256,1280]{1,0:T(8,128)(2,1)} %own.3) | copy-start | bytes 1966084
  119.6 1.1 copy-start
  120.7 29.0 %collective-permute-start.6 = (bf16[256,1280]{1,0:T(8,128)(2,1)}, bf16[256,1280]{1,0:T(8,128)(2,1)}, u32[]{:S(2)}, u32[]{:S(2)}) collective-permute-start(bf16[256,1280]{1,0:T(8,128)(2,1)} %get-tuple-element.23), channel_id=1, source_target_pairs={{0,4},{1,5},{2,6},{3,7},{4,0},{5,1},{6,2},{7,3},{8,12},{9,13},{10,... | collective-permute-start | bytes 1966088 | tf_op jit(solution)/shard_map/ppermute | solution.py:45
  120.9 15.3 %collective-permute-start.10 = (bf16[256,512]{1,0:T(8,128)(2,1)S(1)}, bf16[256,512]{1,0:T(8,128)(2,1)S(1)}, u32[]{:S(2)}, u32[]{:S(2)}) collective-permute-start(bf16[256,512]{1,0:T(8,128)(2,1)S(1)} %get-tuple-element.27), channel_id=1, source_target_pairs={{0,5},{1,0},{2,4},{3,1},{4,7},{5,2},{6,6},{7,3},{8,13},{9,8},{10,1... | collective-permute-start | bytes 786440 | tf_op jit(solution)/shard_map/ppermute | solution.py:45
  125.8 10.5 %collective-permute-start.7 = (bf16[256,512]{1,0:T(8,128)(2,1)S(1)}, bf16[256,512]{1,0:T(8,128)(2,1)S(1)}, u32[]{:S(2)}, u32[]{:S(2)}) collective-permute-start(bf16[256,512]{1,0:T(8,128)(2,1)S(1)} %get-tuple-element.24), channel_id=1, source_target_pairs={{0,0},{1,4},{2,1},{3,5},{4,2},{5,6},{6,3},{7,7},{8,8},{9,12},{10,9... | collective-permute-start | bytes 786440 | tf_op jit(solution)/shard_map/ppermute | solution.py:45
  127.9 8.4 %collective-permute-start.8 = (bf16[256,512]{1,0:T(8,128)(2,1)S(1)}, bf16[256,512]{1,0:T(8,128)(2,1)S(1)}, u32[]{:S(2)}, u32[]{:S(2)}) collective-permute-start(bf16[256,512]{1,0:T(8,128)(2,1)S(1)} %get-tuple-element.25), channel_id=1, source_target_pairs={{0,4},{1,1},{2,5},{3,0},{4,6},{5,3},{6,7},{7,2},{8,12},{9,9},{10,1... | collective-permute-start | bytes 786440 | tf_op jit(solution)/shard_map/ppermute | solution.py:45
  128.6 12.1 %collective-permute-start.9 = (bf16[256,512]{1,0:T(8,128)(2,1)S(1)}, bf16[256,512]{1,0:T(8,128)(2,1)S(1)}, u32[]{:S(2)}, u32[]{:S(2)}) collective-permute-start(bf16[256,512]{1,0:T(8,128)(2,1)S(1)} %get-tuple-element.26), channel_id=1, source_target_pairs={{0,1},{1,5},{2,0},{3,4},{4,3},{5,7},{6,2},{7,6},{8,9},{9,13},{10,8... | collective-permute-start | bytes 786440 | tf_op jit(solution)/shard_map/ppermute | solution.py:45
  130.4 1.0 copy-start.1
  132.7 12.7 %copy-start.3 = (s32[2]{0:T(128)S(1)}, s32[2]{0:T(128)}, u32[]{:S(2)}) copy-start(s32[2]{0:T(128)} %copy-done.2) | copy-start | bytes 28
  132.7 12.7 %all-to-all-start.2 = ((bf16[4,80,512]{2,1,0:T(8,128)(2,1)}), bf16[4,80,512]{2,1,0:T(8,128)(2,1)S(1)}, u32[]{:S(2)}, u32[]{:S(2)}) async-start(bf16[4,80,512]{2,1,0:T(8,128)(2,1)} %shard_map.106), calls=%async_computation.3 | async-start | bytes 655360 | tf_op jit(solution)/shard_map/all_to_all | solution.py:49
  136.3 5.1 %copy-start.6 = (bf16[256,512]{1,0:T(8,128)(2,1)}, bf16[256,512]{1,0:T(8,128)(2,1)S(1)}, u32[]{:S(2)}) copy-start(bf16[256,512]{1,0:T(8,128)(2,1)S(1)} %collective-permute-done.10.a3) | copy-start | bytes 786436
  136.3 5.1 %copy-start.7 = (bf16[256,512]{1,0:T(8,128)(2,1)}, bf16[256,512]{1,0:T(8,128)(2,1)S(1)}, u32[]{:S(2)}) copy-start(bf16[256,512]{1,0:T(8,128)(2,1)S(1)} %collective-permute-done.7.a0) | copy-start | bytes 786436
  136.3 4.3 %copy-start.8 = (bf16[256,512]{1,0:T(8,128)(2,1)}, bf16[256,512]{1,0:T(8,128)(2,1)S(1)}, u32[]{:S(2)}) copy-start(bf16[256,512]{1,0:T(8,128)(2,1)S(1)} %collective-permute-done.8.a1) | copy-start | bytes 786436
  140.7 0.7 copy-start.9
  146.0 9.4 %collective-permute-start.11 = (bf16[80,512]{1,0:T(8,128)(2,1)S(1)}, bf16[80,512]{1,0:T(8,128)(2,1)S(1)}, u32[]{:S(2)}, u32[]{:S(2)}) collective-permute-start(bf16[80,512]{1,0:T(8,128)(2,1)S(1)} %shard_map.107), channel_id=1, source_target_pairs={{0,0},{1,64},{2,128},{3,192},{4,2},{5,66},{6,130},{7,194},{8,8},{9... | collective-permute-start | bytes 245768 | tf_op jit(solution)/shard_map/ppermute | solution.py:45
Sparse Core Ops, SparseCore 0:
  32.2 62.2 reduce-scatter.1
